TPU v7x, 128 devices: a whole 4x4x4 slice. The times are simulated.
128 devices in a mesh: rows: 32 (over z, y, core), hosts: 4 (over x).
Axes of the slice: x: 4, y: 4, z: 4, core: 2. Of those that a mesh axis runs over, the one named last changes fastest.
Arguments:
- embeddings: float32 [131072, 768], P(('rows', 'hosts')), may hold values from -6 to 6
- root_centroids: float32 [512, 768], replicated, may hold values from -6 to 6
- member_ids: int32 [3, 131072], P(None, ('rows', 'hosts')), may hold values from 0 to 511
- split_order: int32 [3, 512], replicated, may hold values from 0 to 511, each once within a row
- seed_rows: int32 [3, 256, 2], replicated, may hold values from 0 to 131071
Outputs:
- centroids: float32 [512, 768], replicated
- spread: float32 [3, 512], replicated
- child_weight: float32 [3, 131072], P(None, ('rows', 'hosts'))
Inputs may be any that keep to these rules, and one draw needn't show every extreme that they name: Each row of split_order names every cluster number once; its first 256 entries are the clusters split at that level.
All inputs are finite; a program needn't handle non-finite values.
Results may differ from a plain program's by a relative error of at most 0.0003.
Values sent between devices are 32-bit elements; how exact they have to be, the bound alone decides.
A program may use at most 64 MiB of HBM per device.

v0:
```python
import math

import jax
import jax.numpy as jnp
from jax import lax
from jax.sharding import Mesh
from jax.sharding import PartitionSpec as P

ROWS = ("rows_0", "rows_1", "rows_2")
ROWS_HOSTS = ("rows_0", "rows_1", "rows_2", "hosts")


def split_up(value, dim, peers):
    lengths = value.shape
    parts = value.reshape(*lengths[:dim], peers, lengths[dim] // peers, *lengths[dim + 1 :])
    return jnp.moveaxis(parts, dim, 0)


def sum_at_owner(value, axis, dim):
    parts = split_up(value, dim, lax.axis_size(axis))
    arrived = lax.all_to_all(parts, axis, split_axis=0, concat_axis=0, tiled=True)
    return arrived.sum(axis=0)


def sum_in_two_steps(value, axes, dim):
    far, near = axes
    own = sum_at_owner(split_up(value, dim, lax.axis_size(far)), near, dim + 1)
    return jnp.sum(lax.all_to_all(own, far, 0, 0, tiled=True), axis=0)


def in_one_piece(arrays, axis, dim, along):
    widths = [math.prod(a.shape[along:]) for a in arrays]
    both = jnp.concatenate(
        [a.reshape(*a.shape[:along], w) for a, w in zip(arrays, widths)], axis=along
    )
    result = sum_in_two_steps(both, axis, dim)
    parts = jnp.split(result, [sum(widths[:k]) for k in range(1, len(widths))], axis=along)
    return tuple(
        (b.reshape(*result.shape[:along], *a.shape[along:]) for a, b in zip(arrays, parts))
    )


def sent_to_all(value, axis):
    copies = jnp.broadcast_to(value, (lax.axis_size(axis), *value.shape))
    return lax.all_to_all(copies, axis, split_axis=0, concat_axis=0, tiled=True)


def joined_along(parts, dim):
    lengths = list(parts.shape[1:])
    lengths[dim] *= parts.shape[0]
    return jnp.moveaxis(parts, 0, dim).reshape(lengths)


def gather_axes(value, axes, dim):
    far, near = axes
    parts = sent_to_all(sent_to_all(value, far), near)
    return joined_along(parts.swapaxes(0, 1).reshape(-1, *value.shape), dim)


def in_one_piece_2(arrays, axis, dim, along):
    widths = [math.prod(a.shape[along:]) for a in arrays]
    both = jnp.concatenate(
        [a.reshape(*a.shape[:along], w) for a, w in zip(arrays, widths)], axis=along
    )
    result = gather_axes(both, axis, dim)
    parts = jnp.split(result, [sum(widths[:k]) for k in range(1, len(widths))], axis=along)
    return tuple(
        (b.reshape(*result.shape[:along], *a.shape[along:]) for a, b in zip(arrays, parts))
    )


def finish(sums, counts, energy, seeds_flat, width):
    centre = (sums + seeds_flat) / (counts + 1.0)[:, None]
    error = (
        energy - 2.0 * jnp.sum(centre * sums, axis=1) + counts * jnp.sum(centre * centre, axis=1)
    )
    return (centre, error / ((counts + 1.0) * width))


def on_device(embeddings, root_centroids, member_ids, split_order, seed_rows):
    high = lax.Precision.HIGHEST
    rows_dev, width = embeddings.shape
    splits_count = seed_rows.shape[1]
    clusters = 2 * splits_count
    devices = lax.axis_size(ROWS) * lax.axis_size("hosts")
    position = lax.axis_index(ROWS) * lax.axis_size("hosts") + lax.axis_index("hosts")
    first_row = position * rows_dev
    scale = 0.5 / jnp.sqrt(jnp.float32(width))
    squares = jnp.sum(embeddings * embeddings, axis=1)
    local = seed_rows - first_row
    local_inside = (local >= 0) & (local < rows_dev)
    picked = jnp.take(embeddings, jnp.clip(local, 0, rows_dev - 1), axis=0)
    fetched_all = lax.psum(jnp.where(local_inside[..., None], picked, jnp.float32(0.0)), ROWS_HOSTS)
    current = root_centroids
    spreads = []
    weights_out = []
    for level in range(seed_rows.shape[0]):
        splits = split_order[level, :splits_count]
        parent = jnp.take(current, splits, axis=0)
        fetched = fetched_all[level]
        seeds = 0.5 * (parent[:, None, :] + fetched)
        delta = seeds[:, 0, :] - seeds[:, 1, :]
        offset = jnp.sum(seeds[:, 1, :] ** 2, axis=1) - jnp.sum(seeds[:, 0, :] ** 2, axis=1)
        chosen = (member_ids[level][:, None] == splits[None, :]).astype(jnp.float32)
        projected = lax.dot_general(embeddings, delta, (((1,), (1,)), ((), ())), precision=high)
        gap = jnp.sum(chosen * (2.0 * projected + offset[None, :]), axis=1)
        first = jax.nn.sigmoid(gap * scale)
        inside = jnp.sum(chosen, axis=1)
        weights_out.append(first * inside)
        weights = jnp.stack([chosen * first[:, None], chosen * (1.0 - first)[:, None]], axis=2)
        weights = weights.reshape(rows_dev, clusters)
        sums = lax.dot_general(weights, embeddings, (((0,), (0,)), ((), ())), precision=high)
        counts = jnp.sum(weights, axis=0)
        energy = jnp.dot(squares, weights, precision=high)
        seeds_flat = seeds.reshape(clusters, width)
        share_sums, share_counts, share_energy = in_one_piece(
            (sums, counts, energy), (("rows_0", "rows_1"), ("rows_2", "hosts")), 0, 1
        )
        share_rows = clusters // devices
        share_seeds = lax.dynamic_slice_in_dim(seeds_flat, position * share_rows, share_rows, 0)
        centre, spread = finish(share_sums, share_counts, share_energy, share_seeds, width)
        current, spread = in_one_piece_2(
            (centre, spread), (("rows_0", "rows_1"), ("rows_2", "hosts")), 0, 1
        )
        spreads.append(spread)
    return (current, jnp.stack(spreads), jnp.stack(weights_out))


def solution(mesh):
    split = Mesh(
        mesh.devices.reshape(4, 4, 2, mesh.shape["hosts"]), ("rows_0", "rows_1", "rows_2", "hosts")
    )
    in_specs = (P(ROWS_HOSTS, None), P(), P(None, ROWS_HOSTS), P(), P())
    out_specs = (P(), P(), P(None, ROWS_HOSTS))
    return jax.shard_map(
        on_device, mesh=split, in_specs=in_specs, out_specs=out_specs, check_vma=False
    )
```

profile of v0, /device:TPU:1, one launch (start us, length us, event | category | flops | bytes accessed | tf_op | source)
XLA Modules:
  0.0 607.8 jit_solution(12349633619163511583)
XLA Ops:
  9.0 8.6 %gather_fusion = f32[1536,768]{1,0:T(8,128)} fusion(f32[1024,768]{1,0:T(8,128)} %param.7, s32[2048]{0:T(1024)S(1)} %pad_clamp_fusion), kind=kCustom, calls=%fused_computation.3 | custom fusion | bytes 9443328 | tf_op jit(solution)/shard_map/jit(_take)/gather | solution.py:92
  17.6 6.8 %reshape.774 = f32[3,256,2,768]{3,2,1,0:T(2,128)} reshape(f32[1536,768]{1,0:T(8,128)} %gather_fusion) | data formatting | bytes 9437184 | tf_op jit(solution)/shard_map/jit(_take)/gather | solution.py:92
  24.4 7.3 %select_select_fusion = f32[3,256,2,768]{3,2,1,0:T(2,128)} fusion(f32[3,256,2,768]{3,2,1,0:T(2,128)} %reshape.774, pred[3,256,2]{2,1,0:T(8,128)(4,1)S(1)} %copy.104, pred[3,256,2]{2,1,0:T(8,128)(4,1)S(1)} %copy.103), kind=kLoop, calls=%fused_computation.4 | loop fusion | flops 2359296 | bytes 9440256 | tf_op jit(solution)/shard_map/jit(_where)/select_n | solution.py:93
  36.2 154.3 %all-reduce.2.cloned.1.call-done = f32[3,256,2,768]{3,2,1,0:T(2,128)} async-done(((f32[3,256,2,768]{3,2,1,0:T(2,128)}), f32[3,256,2,768]{3,2,1,0:T(2,128)}) %all-reduce.2.cloned.1.call-update) | async-done | bytes 4718608 | tf_op jit(solution)/shard_map/psum | solution.py:93
  193.1 3.3 multiply_reduce_fusion.5
  196.4 2.9 fusion.27
  201.0 3.4 fusion.65
  205.4 3.9 reshape.737
  209.3 2.9 dot_general.47
  212.2 8.9 %fusion.4 = f32[16,8,4,768]{3,1,2,0:T(8,128)S(1)} fusion(f32[1024,768]{1,0:T(8,128)} %param.7, f32[16,8,4,1024]{3,2,1,0:T(4,128)} %dot_general.47), kind=kOutput, calls=%fused_computation.15 | convolution fusion | flops 4831838208 | bytes 6815744 | tf_op jit(solution)/shard_map/dot_general | solution.py:112
  221.1 2.6 fusion.10
  226.3 15.8 %all-to-all-start = ((f32[8,16,4,770]{3,2,1,0:T(4,128)}), f32[8,16,4,770]{3,2,1,0:T(4,128)S(1)}, u32[]{:S(2)}, u32[]{:S(2)}) async-start(f32[8,16,4,770]{3,2,1,0:T(4,128)} %copy.109), calls=%async_computation | async-start | bytes 3670016 | tf_op jit(solution)/shard_map/all_to_all | solution.py:21
  243.9 3.1 add.209
  247.0 18.5 %all-to-all-done = f32[8,16,4,770]{3,2,1,0:T(4,128)S(1)} async-done(((f32[8,16,4,770]{3,2,1,0:T(4,128)}), f32[8,16,4,770]{3,2,1,0:T(4,128)S(1)}, u32[]{:S(2)}, u32[]{:S(2)}) %all-to-all-start) | async-done | bytes 1576992 | tf_op jit(solution)/shard_map/all_to_all | solution.py:21
  266.6 4.3 all-to-all-start.1
  271.0 4.4 fusion.66
  280.3 11.6 %all_to_all.60 = f32[16,4,769]{2,1,0:T(4,128)S(1)} all-to-all(f32[16,4,769]{2,1,0:T(4,128)S(1)} %broadcast_in_dim.72), channel_id=1, replica_groups=mesh['rows_0'=4,'rows_1'=4,'rows_2'=2,'hosts'=4] {'rows_0','rows_1'}, dimensions={0} | all-to-all | bytes 393728 | tf_op jit(solution)/shard_map/all_to_all | solution.py:45
  293.4 5.7 all-to-all-start.3
  299.3 23.2 %all-to-all-done.3 = f32[8,16,4,769]{3,2,1,0:T(4,128)S(1)} async-done(((f32[8,16,4,769]{3,2,1,0:T(4,128)}), f32[8,16,4,769]{3,2,1,0:T(4,128)S(1)}, u32[]{:S(2)}, u32[]{:S(2)}) %all-to-all-start.3) | async-done | bytes 1574944 | tf_op jit(solution)/shard_map/all_to_all | solution.py:45
  331.9 3.3 multiply_reduce_fusion.3
  335.3 2.9 fusion.28
  339.9 3.4 fusion.63
  343.3 3.7 reshape.738
  346.9 3.3 dot_general.53
  350.2 4.4 fusion.8
  354.6 9.4 %fusion.2 = f32[16,8,4,768]{3,1,2,0:T(8,128)} fusion(f32[1024,768]{1,0:T(8,128)} %param.7, f32[16,8,4,1024]{3,2,1,0:T(4,128)S(1)} %copy-done.7), kind=kOutput, calls=%fused_computation.13 | convolution fusion | flops 4831838208 | bytes 6815744 | tf_op jit(solution)/shard_map/dot_general | solution.py:112
  367.7 26.8 %all_to_all.61 = f32[8,16,4,770]{3,2,1,0:T(4,128)} all-to-all(f32[8,16,4,770]{3,2,1,0:T(4,128)S(1)} %copy.117), channel_id=1, replica_groups=mesh['rows_0'=4,'rows_1'=4,'rows_2'=2,'hosts'=4] {'rows_2','hosts'}, dimensions={0} | all-to-all | bytes 3153920 | tf_op jit(solution)/shard_map/all_to_all | solution.py:21
  397.1 4.4 all-to-all-start.5
  401.4 3.2 squeeze.15
  411.9 13.0 %all_to_all.62 = f32[16,4,769]{2,1,0:T(4,128)S(1)} all-to-all(f32[16,4,769]{2,1,0:T(4,128)S(1)} %broadcast_in_dim.74), channel_id=1, replica_groups=mesh['rows_0'=4,'rows_1'=4,'rows_2'=2,'hosts'=4] {'rows_0','rows_1'}, dimensions={0} | all-to-all | bytes 393728 | tf_op jit(solution)/shard_map/all_to_all | solution.py:45
  426.4 6.3 %all-to-all-start.7 = ((f32[8,16,4,769]{3,2,1,0:T(4,128)}), f32[8,16,4,769]{3,2,1,0:T(4,128)}, u32[]{:S(2)}, u32[]{:S(2)}) async-start(f32[8,16,4,769]{3,2,1,0:T(4,128)} %broadcast_in_dim.75), calls=%async_computation.7 | async-start | bytes 3670016 | tf_op jit(solution)/shard_map/all_to_all | solution.py:45
  432.9 23.3 %all-to-all-done.7 = f32[8,16,4,769]{3,2,1,0:T(4,128)} async-done(((f32[8,16,4,769]{3,2,1,0:T(4,128)}), f32[8,16,4,769]{3,2,1,0:T(4,128)}, u32[]{:S(2)}, u32[]{:S(2)}) %all-to-all-start.7) | async-done | bytes 1574944 | tf_op jit(solution)/shard_map/all_to_all | solution.py:45
  456.2 3.0 copy.121
  459.2 2.9 reshape_reshape.13
  469.4 3.3 multiply_reduce_fusion.1
  472.8 2.9 fusion.29
  477.4 3.3 fusion.61
  480.7 3.7 reshape.739
  484.4 3.0 dot_general.59
  487.4 4.4 fusion.6
  491.8 9.3 %fusion = f32[16,8,4,768]{3,1,2,0:T(8,128)} fusion(f32[1024,768]{1,0:T(8,128)} %param.7, f32[16,8,4,1024]{3,2,1,0:T(4,128)S(1)} %copy-done.5), kind=kOutput, calls=%fused_computation.11 | convolution fusion | flops 4831838208 | bytes 6815744 | tf_op jit(solution)/shard_map/dot_general | solution.py:112
  504.9 26.8 %all_to_all.63 = f32[8,16,4,770]{3,2,1,0:T(4,128)} all-to-all(f32[8,16,4,770]{3,2,1,0:T(4,128)S(1)} %copy.125), channel_id=1, replica_groups=mesh['rows_0'=4,'rows_1'=4,'rows_2'=2,'hosts'=4] {'rows_2','hosts'}, dimensions={0} | all-to-all | bytes 3153920 | tf_op jit(solution)/shard_map/all_to_all | solution.py:21
  534.2 4.4 all-to-all-start.9
  538.7 3.2 squeeze.17
  549.2 13.0 %all_to_all.64 = f32[16,4,769]{2,1,0:T(4,128)S(1)} all-to-all(f32[16,4,769]{2,1,0:T(4,128)S(1)} %broadcast_in_dim.76), channel_id=1, replica_groups=mesh['rows_0'=4,'rows_1'=4,'rows_2'=2,'hosts'=4] {'rows_0','rows_1'}, dimensions={0} | all-to-all | bytes 393728 | tf_op jit(solution)/shard_map/all_to_all | solution.py:45
  563.6 6.2 %all-to-all-start.11 = ((f32[8,16,4,769]{3,2,1,0:T(4,128)}), f32[8,16,4,769]{3,2,1,0:T(4,128)}, u32[]{:S(2)}, u32[]{:S(2)}) async-start(f32[8,16,4,769]{3,2,1,0:T(4,128)} %broadcast_in_dim.77), calls=%async_computation.11 | async-start | bytes 3670016 | tf_op jit(solution)/shard_map/all_to_all | solution.py:45
  571.8 21.6 %all-to-all-done.11 = f32[8,16,4,769]{3,2,1,0:T(4,128)} async-done(((f32[8,16,4,769]{3,2,1,0:T(4,128)}), f32[8,16,4,769]{3,2,1,0:T(4,128)}, u32[]{:S(2)}, u32[]{:S(2)}) %all-to-all-start.11) | async-done | bytes 1574944 | tf_op jit(solution)/shard_map/all_to_all | solution.py:45
  593.4 3.0 copy.129
  (128 shorter events, 79.6 us)
Async XLA Ops:
  7.2 25.4 %copy-start = (f32[512,768]{1,0:T(8,128)S(1)}, f32[512,768]{1,0:T(8,128)}, u32[]{:S(2)}) copy-start(f32[512,768]{1,0:T(8,128)} %param.8) | copy-start | bytes 4718596
  7.2 183.3 %all-reduce.2.cloned.1.call-start = ((), (), s32[]{:S(2)}) async-start(), calls=%async_computation.12 | async-start | bytes 9437184 | tf_op jit(solution)/shard_map/psum | solution.py:93
  32.6 1.1 copy-start.8
  190.5 5.9 copy-start.2
  212.2 8.9 %copy-start.6 = (f32[16,8,4,1024]{3,2,1,0:T(4,128)S(1)}, f32[16,8,4,1024]{3,2,1,0:T(4,128)}, u32[]{:S(2)}) copy-start(f32[16,8,4,1024]{3,2,1,0:T(4,128)} %dot_general.47) | copy-start | bytes 6291460
  226.3 39.2 %all-to-all-start = ((f32[8,16,4,770]{3,2,1,0:T(4,128)}), f32[8,16,4,770]{3,2,1,0:T(4,128)S(1)}, u32[]{:S(2)}, u32[]{:S(2)}) async-start(f32[8,16,4,770]{3,2,1,0:T(4,128)} %copy.109), calls=%async_computation | async-start | bytes 3670016 | tf_op jit(solution)/shard_map/all_to_all | solution.py:21
  266.6 12.2 %all-to-all-start.1 = ((f32[16,4,770]{2,1,0:T(4,128)}), f32[16,4,770]{2,1,0:T(4,128)S(1)}, u32[]{:S(2)}, u32[]{:S(2)}) async-start(f32[16,4,770]{2,1,0:T(4,128)} %reduce_sum.269), calls=%async_computation.1 | async-start | bytes 458752 | tf_op jit(solution)/shard_map/all_to_all | solution.py:28
  293.4 29.1 %all-to-all-start.3 = ((f32[8,16,4,769]{3,2,1,0:T(4,128)}), f32[8,16,4,769]{3,2,1,0:T(4,128)S(1)}, u32[]{:S(2)}, u32[]{:S(2)}) async-start(f32[8,16,4,769]{3,2,1,0:T(4,128)} %broadcast_in_dim.73), calls=%async_computation.3 | async-start | bytes 3670016 | tf_op jit(solution)/shard_map/all_to_all | solution.py:45
  329.3 5.9 copy-start.3
  350.2 4.4 copy-start.7
  397.1 12.5 %all-to-all-start.5 = ((f32[16,4,770]{2,1,0:T(4,128)}), f32[16,4,770]{2,1,0:T(4,128)}, u32[]{:S(2)}, u32[]{:S(2)}) async-start(f32[16,4,770]{2,1,0:T(4,128)} %reduce_sum.278), calls=%async_computation.5 | async-start | bytes 458752 | tf_op jit(solution)/shard_map/all_to_all | solution.py:28
  426.4 29.8 %all-to-all-start.7 = ((f32[8,16,4,769]{3,2,1,0:T(4,128)}), f32[8,16,4,769]{3,2,1,0:T(4,128)}, u32[]{:S(2)}, u32[]{:S(2)}) async-start(f32[8,16,4,769]{3,2,1,0:T(4,128)} %broadcast_in_dim.75), calls=%async_computation.7 | async-start | bytes 3670016 | tf_op jit(solution)/shard_map/all_to_all | solution.py:45
  466.9 5.9 copy-start.4
  487.4 4.4 copy-start.5
  534.2 12.5 %all-to-all-start.9 = ((f32[16,4,770]{2,1,0:T(4,128)}), f32[16,4,770]{2,1,0:T(4,128)}, u32[]{:S(2)}, u32[]{:S(2)}) async-start(f32[16,4,770]{2,1,0:T(4,128)} %reduce_sum.287), calls=%async_computation.9 | async-start | bytes 458752 | tf_op jit(solution)/shard_map/all_to_all | solution.py:28
  563.6 29.8 %all-to-all-start.11 = ((f32[8,16,4,769]{3,2,1,0:T(4,128)}), f32[8,16,4,769]{3,2,1,0:T(4,128)}, u32[]{:S(2)}, u32[]{:S(2)}) async-start(f32[8,16,4,769]{3,2,1,0:T(4,128)} %broadcast_in_dim.77), calls=%async_computation.11 | async-start | bytes 3670016 | tf_op jit(solution)/shard_map/all_to_all | solution.py:45
  596.4 4.1 copy-start.1
Sparse Core Ops, SparseCore 0:
  31.9 158.5 all-reduce.1
where the time goes:
time: 618 us; the launch traced here: 608 us
  waiting for transfers between devices  245 us (40%)
  local copies, waits for them, and re-layouts  98.8 us (16%)
  blocking collectives  91.2 us (15%)
  other arithmetic  62.7 us (10%)
  matrix products  47.6 us (8%)
  starting transfers between devices  47.2 us (8%)
  between operations  15.1 us (2%)
    psum x1, waiting for transfers between devices, on_device(): lax.psum(jnp.where(local_inside[..., None], picked, jnp.float32(0.0)), RO...  154 us
    all_to_all x3, waiting for transfers between devices, sent_to_all(): return lax.all_to_all(copies, axis, split_axis=0, concat_axis=0, tiled=True)  68.1 us
    all_to_all x2, blocking collectives, sum_at_owner(): lax.all_to_all(parts, axis, split_axis=0, concat_axis=0, tiled=True)  53.7 us
    all_to_all x3, blocking collectives, sent_to_all(): return lax.all_to_all(copies, axis, split_axis=0, concat_axis=0, tiled=True)  37.6 us
    dot_general x3, matrix products, on_device(): lax.dot_general(weights, embeddings, (((0,), (0,)), ((), ())), precision=...  27.6 us
    all_to_all x1, waiting for transfers between devices, sum_at_owner(): lax.all_to_all(parts, axis, split_axis=0, concat_axis=0, tiled=True)  18.5 us
    all_to_all x3, starting transfers between devices, sent_to_all(): return lax.all_to_all(copies, axis, split_axis=0, concat_axis=0, tiled=True)  18.2 us
    all_to_all x1, starting transfers between devices, sum_at_owner(): lax.all_to_all(parts, axis, split_axis=0, concat_axis=0, tiled=True)  15.8 us
  transfers between devices with their start and end apart: 8, of which 8 were waited for; matrix products, arithmetic and copies ran while one was open for 5% of the time, Pallas kernels for 0%

commit v1 on v0

v1 whole, which is shorter than its diff:
```python
import jax
import jax.numpy as jnp
from jax import lax
from jax.experimental import pallas as pl
from jax.experimental.pallas import tpu as pltpu
from jax.sharding import Mesh
from jax.sharding import PartitionSpec as P

F32 = jnp.float32
BF = jnp.bfloat16
I32 = jnp.int32
MESH = pl.DeviceIdType.MESH
HIGH = lax.Precision.HIGHEST

AXES = ("z", "y", "c", "x")
SIZE = {"z": 4, "y": 4, "c": 2, "x": 4}
ORDERS = (("x", "y", "z"), ("y", "z", "x"), ("z", "x", "y"))
PARTS = 3
ROWS = 1024
WIDTH = 768
SPLITS = 256
LEVELS = 3
KIDS = 512
TILE = 128


def two(value):
    high = value.astype(BF)
    return high, (value - high.astype(F32)).astype(BF)


def dot(a, b):
    return jnp.dot(a, b, preferred_element_type=F32)


def aligned(value, step):
    return pl.multiple_of(value, step)


class Links:
    def __init__(self):
        self.me = {a: lax.axis_index(a) for a in AXES}
        self.started = []

    def at(self, axis, step):
        return lax.rem(self.me[axis] + step, SIZE[axis])

    def send(self, src, dst, send_sem, recv_sem, device):
        copy = pltpu.make_async_remote_copy(
            src_ref=src, dst_ref=dst, send_sem=send_sem, recv_sem=recv_sem, device_id=device, device_id_type=MESH
        )
        copy.start()
        self.started.append(copy)
        return copy

    def drain(self):
        for copy in self.started:
            copy.wait_send()
        self.started = []


def near_group(links):
    return [{"x": links.at("x", i), "c": links.at("c", j)} for i in range(4) for j in range(2) if i or j]


def far_group(links):
    return [{"z": links.at("z", i), "y": links.at("y", j)} for i in range(4) for j in range(4) if i or j]


class AllSum:
    def __init__(self, links, near, far, sems):
        self.links, self.near, self.far, self.sems = links, near, far, sems

    def start(self, rows):
        links = self.links
        slot = links.me["x"] * 2 + links.me["c"]
        for i, row in enumerate(rows):
            self.near[slot, i : i + 1, :] = row
        if len(rows) < 8:
            self.near[slot, len(rows) :, :] = jnp.zeros((8 - len(rows), SPLITS), F32)
        mine = self.near.at[slot]
        self.waits = [
            links.send(mine, mine, self.sems.at[0, k], self.sems.at[1, k], device)
            for k, device in enumerate(near_group(links))
        ]

    def middle(self):
        links = self.links
        for copy in self.waits:
            copy.wait_recv()
        total = self.near[0]
        for k in range(1, 8):
            total = total + self.near[k]
        slot = links.me["z"] * 4 + links.me["y"]
        self.far[slot] = total
        mine = self.far.at[slot]
        self.waits = [
            links.send(mine, mine, self.sems.at[0, 7 + k], self.sems.at[1, 7 + k], device)
            for k, device in enumerate(far_group(links))
        ]

    def finish(self):
        for copy in self.waits:
            copy.wait_recv()
        total = self.far[0]
        for k in range(1, 16):
            total = total + self.far[k]
        return total


def add_into(dst, first, rows, sources, step):
    @pl.loop(0, rows // step)
    def _(i):
        at = pl.ds(aligned(first + i * step, step), step)
        total = dst[at, :]
        for source in sources:
            total = total + source[pl.ds(aligned(i * step, step), step), :]
        dst[at, :] = total


class Scatter:
    def __init__(self, links, data, core, one, two_, three, sems):
        self.links, self.data, self.sems = links, data, sems
        self.core, self.one, self.two, self.three = core, one, two_, three
        self.waits = None

    def send(self, q, k, src, dst, device):
        return self.links.send(src, dst, self.sems.at[0, q, k], self.sems.at[1, q, k], device)

    def wait(self):
        for copy in self.waits:
            copy.wait_recv()
        self.waits = []

    def start_core(self):
        links = self.links
        c = links.me["c"]
        self.waits = []
        for q in range(PARTS):
            src = self.data.at[pl.ds(aligned(256 * q + 128 * (1 - c), 128), 128), :]
            self.waits.append(self.send(q, 0, src, self.core.at[q], {"c": 1 - c}))

    def start_one(self):
        links = self.links
        self.wait()
        for q in range(PARTS):
            base = 256 * q + 128 * links.me["c"]
            add_into(self.data, base, 128, [self.core.at[q]], 16)
            axis = ORDERS[q][0]
            for k in range(1, 4):
                other = links.at(axis, k)
                src = self.data.at[pl.ds(aligned(base + 32 * other, 32), 32), :]
                self.waits.append(self.send(q, k, src, self.one.at[q, k - 1], {axis: other}))

    def start_two(self):
        links = self.links
        self.wait()
        for q in range(PARTS):
            base = 256 * q + 128 * links.me["c"] + 32 * links.me[ORDERS[q][0]]
            add_into(self.data, base, 32, [self.one.at[q, k] for k in range(3)], 8)
            axis = ORDERS[q][1]
            for k in range(1, 4):
                other = links.at(axis, k)
                src = self.data.at[pl.ds(aligned(base + 8 * other, 8), 8), :]
                self.waits.append(self.send(q, 3 + k, src, self.two.at[q, k - 1], {axis: other}))

    def start_three(self):
        links = self.links
        self.wait()
        for q in range(PARTS):
            base = own_row(links, q)
            axis = ORDERS[q][2]
            slot = links.me[axis]
            total = self.data[pl.ds(aligned(base, 8), 8), :]
            for k in range(3):
                total = total + self.two[q, k]
            self.three[q, slot] = total
            mine = self.three.at[q, slot]
            for k in range(1, 4):
                self.waits.append(self.send(q, 6 + k, mine, mine, {axis: links.at(axis, k)}))

    def finish(self):
        self.wait()
        return [
            ((self.three[q, 0] + self.three[q, 1]) + self.three[q, 2]) + self.three[q, 3] for q in range(PARTS)
        ]


def own_row(links, q):
    first, second, _ = ORDERS[q]
    return 256 * q + 128 * links.me["c"] + 32 * links.me[first] + 8 * links.me[second]


class Gather:
    def __init__(self, links, data, sems):
        self.links, self.data, self.sems = links, data, sems

    def push(self, q, k, base, rows, device):
        block = self.data.at[pl.ds(aligned(base, rows), rows), :]
        return self.links.send(block, block, self.sems.at[0, q, k], self.sems.at[1, q, k], device)

    def wait(self):
        for copy in self.waits:
            copy.wait_recv()
        self.waits = []

    def start_two(self, own):
        links = self.links
        self.waits = []
        for q in range(PARTS):
            base = own_row(links, q)
            self.data[pl.ds(aligned(base, 8), 8), :] = own[q]
            axis = ORDERS[q][1]
            for k in range(1, 4):
                self.waits.append(self.push(q, k, base, 8, {axis: links.at(axis, k)}))

    def start_one(self):
        links = self.links
        self.wait()
        for q in range(PARTS):
            base = 256 * q + 128 * links.me["c"] + 32 * links.me[ORDERS[q][0]]
            axis = ORDERS[q][0]
            for k in range(1, 4):
                self.waits.append(self.push(q, 3 + k, base, 32, {axis: links.at(axis, k)}))

    def start_core(self):
        links = self.links
        self.wait()
        c = links.me["c"]
        for q in range(PARTS):
            self.waits.append(self.push(q, 0, 256 * q + 128 * c, 128, {"c": 1 - c}))

    def finish(self):
        self.wait()


def pick(index, columns):
    hit = lax.broadcasted_iota(I32, (SPLITS, SPLITS), 0) == index
    return [jnp.sum(jnp.where(hit, column, 0), axis=0, keepdims=True) for column in columns]


def kernel(e_ref, root_ref, mem_ref, tabr_ref, tabc_ref, cent_ref, spread_ref, cw_ref, *scratch):
    (
        eh, el, eth, etl, rh, rl, roott, oh, w_lo, dh, dl, proj, sq, cwbuf,
        xd, x0, x1, x2, df, cf,
        core_d, core_0, core_1, core_2,
        one_d, one_0, one_1, one_2,
        two_d, two_0, two_1, two_2,
        three_d, three_0, three_1, three_2,
        near, far, woven, sem_rs, sem_ag, sem_ar,
    ) = scratch
    w_hi = oh
    links = Links()
    me = links.me
    barrier = pltpu.get_barrier_semaphore()
    peers = near_group(links) + far_group(links)
    for device in peers:
        pl.semaphore_signal(barrier, inc=1, device_id=device, device_id_type=MESH)

    rs_d = Scatter(links, xd, core_d, one_d, two_d, three_d, sem_rs.at[0])
    rs_0 = Scatter(links, x0, core_0, one_0, two_0, three_0, sem_rs.at[1])
    rs_1 = Scatter(links, x1, core_1, one_1, two_1, three_1, sem_rs.at[2])
    rs_2 = Scatter(links, x2, core_2, one_2, two_2, three_2, sem_rs.at[3])
    ag_d = Gather(links, df, sem_ag.at[0])
    ag_c = Gather(links, cf, sem_ag.at[1])
    sums = [AllSum(links, near.at[i], far.at[i], sem_ar.at[i]) for i in range(5)]

    first_row = (me["z"] * 32 + me["y"] * 8 + me["c"] * 4 + me["x"]) * ROWS

    @pl.loop(0, ROWS // TILE)
    def _(i):
        at = pl.ds(aligned(i * TILE, TILE), TILE)
        rows = e_ref[at, :]
        high, low = two(rows)
        eh[at, :] = high
        el[at, :] = low
        sq[at, :] = jnp.sum(rows * rows, axis=1, keepdims=True)
        turned = jnp.transpose(rows)
        high, low = two(turned)
        eth[:, at] = high
        etl[:, at] = low

    splits = [tabr_ref[l : l + 1, :] for l in range(LEVELS)]
    seed = [[tabr_ref[3 + 3 * j + l : 4 + 3 * j + l, :] - first_row for j in range(2)] for l in range(LEVELS)]

    def place(sign, with_norm):
        zero = jnp.zeros((1, SPLITS), F32)

        def body(i, carry):
            at = pl.ds(aligned(i * TILE, TILE), TILE)
            row = lax.broadcasted_iota(I32, (TILE, SPLITS), 0) + i * TILE
            out = []
            for l in range(LEVELS):
                value = jnp.where(row == seed[l][0], 1.0, 0.0) + jnp.where(row == seed[l][1], sign, 0.0)
                oh[at, l * SPLITS : (l + 1) * SPLITS] = value.astype(BF)
                if with_norm:
                    out.append(carry[l] + jnp.sum(value * sq[at, :], axis=0, keepdims=True))
            return tuple(out) if with_norm else carry

        return lax.fori_loop(0, ROWS // TILE, body, (zero,) * LEVELS)

    def select_rows(dst, first_col):
        @pl.loop(0, WIDTH // 256)
        def _(i):
            at = pl.ds(aligned(i * 256, 256), 256)
            dst[at, first_col : first_col + WIDTH] = dot(eth[at, :], oh[...]) + dot(etl[at, :], oh[...])

    norms = place(-1.0, True)
    select_rows(xd, 0)

    pl.semaphore_wait(barrier, len(peers))
    rs_d.start_core()
    sums[0].start(list(norms))

    col = [tabc_ref[:, k : k + 1] for k in range(6)]
    kid1 = splits[1]
    a1, s10, s11 = pick(kid1 >> 1, [col[0], col[2], col[3]])
    odd1 = (kid1 & 1) == 1
    seed1 = jnp.where(odd1, s11, s10) - first_row
    kid2 = splits[2]
    mid2, s20, s21 = pick(kid2 >> 1, [col[1], col[4], col[5]])
    odd2 = (kid2 & 1) == 1
    seed2 = jnp.where(odd2, s21, s20) - first_row
    a2, t20, t21 = pick(mid2 >> 1, [col[0], col[2], col[3]])
    odd20 = (mid2 & 1) == 1
    seed20 = jnp.where(odd20, t21, t20) - first_row

    @pl.loop(0, KIDS // TILE)
    def _(i):
        at = pl.ds(aligned(i * TILE, TILE), TILE)
        rows = root_ref[at, :]
        high, low = two(rows)
        rh[at, :] = high
        rl[at, :] = low
        roott[:, at] = jnp.transpose(rows)

    rs_d.start_one()
    place(1.0, False)
    sums[0].middle()
    rs_d.start_two()
    rs_d.start_three()
    own_d = jnp.concatenate(rs_d.finish(), axis=0)
    ag_d.start_two([own_d[8 * q : 8 * q + 8] for q in range(PARTS)])
    ag_d.start_one()
    ag_d.start_core()
    select_rows(x0, KIDS)
    norm = sums[0].finish()
    ag_d.finish()

    @pl.loop(0, WIDTH // TILE)
    def _(i):
        at = pl.ds(aligned(i * TILE, TILE), TILE)
        high, low = two(df[at, :])
        dh[at, :] = high
        dl[at, :] = low

    @pl.loop(0, ROWS // 256)
    def _(i):
        at = pl.ds(aligned(i * 256, 256), 256)
        proj[at, :] = dot(eh[at, :], dh[...]) + dot(eh[at, :], dl[...]) + dot(el[at, :], dh[...])

    def root_body(i, carry):
        at = pl.ds(aligned(i * TILE, TILE), TILE)
        value = dot(rh[at, :], dh[...]) + dot(rh[at, :], dl[...]) + dot(rl[at, :], dh[...])
        row = lax.broadcasted_iota(I32, (TILE, SPLITS), 0) + i * TILE
        return tuple(
            carry[l] + jnp.sum(jnp.where(row == index, value[:, l * SPLITS : (l + 1) * SPLITS], 0.0), axis=0, keepdims=True)
            for l, index in enumerate((splits[0], a1, a2))
        )

    along = lax.fori_loop(0, KIDS // TILE, root_body, (jnp.zeros((1, SPLITS), F32),) * LEVELS)

    scale = 0.5 / float(WIDTH) ** 0.5

    def level(l, offset, chains):
        zero = jnp.zeros((1, SPLITS), F32)

        def body(i, carry):
            at = pl.ds(aligned(i * TILE, TILE), TILE)
            member = mem_ref[at, l : l + 1]
            squares = sq[at, :]
            hit = member == splits[l]
            value = proj[at, l * SPLITS : (l + 1) * SPLITS] + offset
            gap = jnp.sum(jnp.where(hit, value, 0.0), axis=1, keepdims=True)
            inside = jnp.sum(jnp.where(hit, 1.0, 0.0), axis=1, keepdims=True)
            first = lax.logistic(gap * scale)
            second = 1.0 - first
            cwbuf[at, l : l + 1] = first * inside
            out = []
            for j, part in enumerate((first, second)):
                weight = jnp.where(hit, part, 0.0)
                high, low = two(weight)
                w_hi[at, j * SPLITS : (j + 1) * SPLITS] = high
                w_lo[at, j * SPLITS : (j + 1) * SPLITS] = low
                out.append(jnp.sum(weight, axis=0, keepdims=True))
                out.append(jnp.sum(weight * squares, axis=0, keepdims=True))
            row = lax.broadcasted_iota(I32, (TILE, SPLITS), 0) + i * TILE
            for cluster, odd, seed_row, ahead in chains:
                weight = jnp.where(member == cluster, jnp.where(odd, second, first), 0.0)
                both = weight + jnp.where(row == seed_row, 0.5, 0.0)
                out.append(jnp.sum(both * proj[at, ahead * SPLITS : (ahead + 1) * SPLITS], axis=0, keepdims=True))
                out.append(jnp.sum(weight, axis=0, keepdims=True))
            return tuple(a + b for a, b in zip(carry, out))

        return list(lax.fori_loop(0, ROWS // TILE, body, (zero,) * (4 + 2 * len(chains))))

    def add_up(dst):
        @pl.loop(0, WIDTH // 256)
        def _(i):
            at = pl.ds(aligned(i * 256, 256), 256)
            wide = w_hi[:, :KIDS]
            dst[at, :KIDS] = dot(eth[at, :], wide) + dot(etl[at, :], wide) + dot(eth[at, :], w_lo[...])

    offset = -0.5 * along[0] - 0.25 * norm[0:1, :]
    sums[1].start(level(0, offset, [(a1, odd1, seed1, 1), (a2, odd20, seed20, 2)]))
    add_up(x0)
    rs_0.start_core()
    sums[1].middle()
    rs_0.start_one()
    got0 = sums[1].finish()

    parent = (got0[4:5, :] + 0.5 * along[1]) / (got0[5:6, :] + 1.0)
    offset = -0.5 * parent - 0.25 * norm[1:2, :]
    sums[2].start(level(1, offset, [(mid2, odd2, seed2, 2)]))
    add_up(x1)
    rs_1.start_core()
    sums[2].middle()
    rs_0.start_two()
    rs_1.start_one()
    got1 = sums[2].finish()

    older = (got0[6:7, :] + 0.5 * along[2]) / (got0[7:8, :] + 1.0)
    parent = (got1[4:5, :] + 0.5 * older) / (got1[5:6, :] + 1.0)
    offset = -0.5 * parent - 0.25 * norm[2:3, :]
    sums[3].start(level(2, offset, []))
    add_up(x2)
    rs_2.start_core()
    sums[3].middle()
    rs_0.start_three()
    rs_1.start_two()
    rs_2.start_one()
    got2 = sums[3].finish()
    own_0 = jnp.concatenate(rs_0.finish(), axis=0)
    rs_1.start_three()
    rs_2.start_two()

    def rows_of_root():
        return jnp.concatenate([roott[pl.ds(aligned(own_row(links, q), 8), 8), :] for q in range(PARTS)], axis=0)

    def child(l, got, mine, from_, kid):
        line = lax.broadcasted_iota(I32, (KIDS, SPLITS), 0)
        parent = jnp.dot(
            from_, jnp.where(line == kid, 1.0, 0.0).astype(F32), precision=HIGH, preferred_element_type=F32
        )
        up = own_0[:, KIDS + l * SPLITS : KIDS + (l + 1) * SPLITS]
        diff = own_d[:, l * SPLITS : (l + 1) * SPLITS]
        seeds = 0.5 * jnp.concatenate([parent + 0.5 * (up + diff), parent + 0.5 * (up - diff)], axis=1)
        count = jnp.concatenate([got[0:1, :], got[2:3, :]], axis=1)
        centre = (mine + seeds) / (count + 1.0)
        error = jnp.sum(count * centre * centre - 2.0 * centre * mine, axis=0, keepdims=True)
        return centre, 0.25 * error, count

    def flat(kid):
        return (kid & 1) * SPLITS + (kid >> 1)

    c1, err0, n0 = child(0, got0, own_0[:, :KIDS], rows_of_root(), splits[0])
    own_1 = jnp.concatenate(rs_1.finish(), axis=0)
    rs_2.start_three()
    c2, err1, n1 = child(1, got1, own_1, c1, flat(kid1))
    own_2 = jnp.concatenate(rs_2.finish(), axis=0)
    c3, err2, n2 = child(2, got2, own_2, c2, flat(kid2))
    ag_c.start_two([c3[8 * q : 8 * q + 8] for q in range(PARTS)])
    sums[4].start([e[:, j * SPLITS : (j + 1) * SPLITS] for e in (err0, err1, err2) for j in range(2)])
    ag_c.start_one()
    sums[4].middle()
    ag_c.start_core()
    cw_ref[...] = jnp.transpose(cwbuf[...])[0:LEVELS]
    total = sums[4].finish()
    lines = []
    for l, (got, n) in enumerate(((got0, n0), (got1, n1), (got2, n2))):
        energy = jnp.concatenate([got[1:2, :], got[3:4, :]], axis=1)
        error = jnp.concatenate([total[2 * l : 2 * l + 1, :], total[2 * l + 1 : 2 * l + 2, :]], axis=1)
        lines.append((energy + error) / ((n + 1.0) * WIDTH))
    lines.append(jnp.zeros((8 - LEVELS, KIDS), F32))
    line = lax.broadcasted_iota(I32, (KIDS, KIDS), 0)
    kid = lax.broadcasted_iota(I32, (KIDS, KIDS), 1)
    order = jnp.where(line == flat(kid), 1.0, 0.0).astype(F32)
    spread_ref[...] = jnp.dot(
        jnp.concatenate(lines, axis=0), order, precision=HIGH, preferred_element_type=F32
    )[0:LEVELS]
    ag_c.finish()
    for w in range(WIDTH // TILE):
        for j in range(2):
            block = jnp.transpose(cf[w * TILE : (w + 1) * TILE, j * SPLITS : (j + 1) * SPLITS])
            woven[w, pl.ds(j, SPLITS, stride=2), :] = block
        cent_ref[:, w * TILE : (w + 1) * TILE] = woven[w]
    links.drain()


def scratch_shapes():
    vm = pltpu.VMEM
    widths = (WIDTH, KIDS + WIDTH, KIDS, KIDS)
    shapes = [
        vm((ROWS, WIDTH), BF), vm((ROWS, WIDTH), BF), vm((WIDTH, ROWS), BF), vm((WIDTH, ROWS), BF),
        vm((KIDS, WIDTH), BF), vm((KIDS, WIDTH), BF), vm((WIDTH, KIDS), F32),
        vm((ROWS, WIDTH), BF), vm((ROWS, KIDS), BF),
        vm((WIDTH, WIDTH), BF), vm((WIDTH, WIDTH), BF), vm((ROWS, WIDTH), F32),
        vm((ROWS, 1), F32), vm((ROWS, 128), F32),
    ]
    shapes += [vm((WIDTH, n), F32) for n in widths]
    shapes += [vm((WIDTH, WIDTH), F32), vm((WIDTH, KIDS), F32)]
    shapes += [vm((PARTS, 128, n), F32) for n in widths]
    shapes += [vm((PARTS, 3, 32, n), F32) for n in widths]
    shapes += [vm((PARTS, 3, 8, n), F32) for n in widths]
    shapes += [vm((PARTS, 4, 8, n), F32) for n in widths]
    dma = pltpu.SemaphoreType.DMA
    shapes += [vm((5, 8, 8, SPLITS), F32), vm((5, 16, 8, SPLITS), F32)]
    shapes += [vm((WIDTH // TILE, KIDS, TILE), F32)]
    shapes += [dma((4, 2, PARTS, 10)), dma((2, 2, PARTS, 7)), dma((5, 2, 22))]
    return shapes


def on_device(embeddings, root_centroids, member_ids, split_order, seed_rows):
    table = jnp.concatenate(
        [split_order[:, :SPLITS], seed_rows[:, :, 0], seed_rows[:, :, 1], jnp.zeros((7, SPLITS), I32)], axis=0
    )
    columns = jnp.stack(
        [
            split_order[0, :SPLITS], split_order[1, :SPLITS],
            seed_rows[0, :, 0], seed_rows[0, :, 1], seed_rows[1, :, 0], seed_rows[1, :, 1],
        ],
        axis=1,
    )
    member = member_ids.T
    vmem = pl.BlockSpec(memory_space=pltpu.VMEM)
    return pl.pallas_call(
        kernel,
        out_shape=(
            jax.ShapeDtypeStruct((KIDS, WIDTH), F32),
            jax.ShapeDtypeStruct((LEVELS, KIDS), F32),
            jax.ShapeDtypeStruct((LEVELS, ROWS), F32),
        ),
        in_specs=[vmem] * 5,
        out_specs=(vmem,) * 3,
        scratch_shapes=scratch_shapes(),
        compiler_params=pltpu.CompilerParams(
            collective_id=0, has_side_effects=True, vmem_limit_bytes=66_000_000
        ),
    )(embeddings, root_centroids, member, table, columns)


def solution(mesh):
    split = Mesh(mesh.devices.reshape(4, 4, 2, 4), AXES)
    everywhere = ("z", "y", "c", "x")
    in_specs = (P(everywhere, None), P(), P(None, everywhere), P(), P())
    out_specs = (P(), P(), P(None, everywhere))
    return jax.shard_map(on_device, mesh=split, in_specs=in_specs, out_specs=out_specs, check_vma=False)
```

time: 618 us -> 132 us (0.21); the launches traced: 608 us -> 132 us
  waiting for transfers between devices: 245 us -> 0 us
  Pallas kernels: 0 us -> 121 us
  blocking collectives: 91.2 us -> 0 us
  local copies, waits for them, and re-layouts: 98.8 us -> 9.51 us
  other arithmetic: 62.7 us -> 0.68 us
  matrix products: 47.6 us -> 0 us
  starting transfers between devices: 47.2 us -> 0 us
  between operations: 15.1 us -> 0.67 us
    psum x1 -> x0, waiting for transfers between devices: 154 us -> none  [on_device(): lax.psum(jnp.where(local_inside[..., None], picked, jnp.float32(0.0)), RO...]
    pallas_call x0 -> x1, Pallas kernels: none -> 121 us  [on_device(): pl.pallas_call(kernel, out_shape=(jax.ShapeDtypeStruct((KIDS, WIDTH), F32...]
    all_to_all x5 -> x0, blocking collectives: 91.2 us -> none  [the longest x2 53.7 us: sum_at_owner(): lax.all_to_all(parts, axis, split_axis=0, concat_axis=0, tiled=True)]
    all_to_all x7 -> x0, waiting for transfers between devices: 90.8 us -> none  [the longest x3 68.1 us: sent_to_all(): return lax.all_to_all(copies, axis, split_axis=0, concat_axis=0, tiled=True)]
    dot_general x9 -> x0, matrix products: 47.6 us -> none  [the longest x3 27.6 us: on_device(): lax.dot_general(weights, embeddings, (((0,), (0,)), ((), ())), precision=...]
    all_to_all x7 -> x0, starting transfers between devices: 47.2 us -> none  [the longest x3 18.2 us: sent_to_all(): return lax.all_to_all(copies, axis, split_axis=0, concat_axis=0, tiled=True)]
    reduce_sum x19 -> x0, other arithmetic: 33.7 us -> none  [the longest x3 10.1 us: on_device(): counts = jnp.sum(weights, axis=0)]
    gather x5 -> x0, local copies, waits for them, and re-layouts: 20.5 us -> none  [the longest x2 15.4 us: on_device(): picked = jnp.take(embeddings, jnp.clip(local, 0, rows_dev - 1), axis=0)]
  transfers between devices with their start and end apart: 8 -> 0, of which waited for: 8 -> 0; matrix products, arithmetic and copies ran while one was open for 5% -> 0% of each run, Pallas kernels for 0% -> 0%
where the time goes in v1:
time: 132 us
  Pallas kernels  121 us (92%)
  local copies, waits for them, and re-layouts  9.51 us (7%)
    pallas_call x1, Pallas kernels, on_device(): pl.pallas_call(kernel, out_shape=(jax.ShapeDtypeStruct((KIDS, WIDTH), F32...  121 us
    unnamed x8, local copies, waits for them, and re-layouts  5.61 us

profile of v1, /device:TPU:1, one launch (start us, length us, event | category | flops | bytes accessed | tf_op | source)
XLA Modules:
  0.0 131.6 jit_solution(13975461125302931663)
XLA Ops:
  0.6 0.1 pad.3.clone
  0.7 0.8 slice_bitcast_fusion.4
  1.5 0.7 slice.27
  2.2 0.8 slice_bitcast_fusion
  3.0 0.8 fusion
  3.7 0.7 add_add_fusion.tabr_ref
  4.4 0.8 copy.23.tabc_ref
  5.2 1.7 %copy.20 = s32[3,1024]{0,1:T(8,128)} copy(s32[3,1024]{1,0:T(4,128)} %param.7) | data formatting | bytes 24576 | tf_op args[2]
  7.0 120.7 %shard_map.76 = (f32[512,768]{1,0:T(8,128)}, f32[3,512]{1,0:T(4,128)}, f32[3,1024]{1,0:T(4,128)}) custom-call(f32[1024,768]{1,0:T(8,128)} %e_ref.1, f32[512,768]{1,0:T(8,128)} %root_ref.1, s32[1024,3]{1,0:T(8,128)} %bitcast.17, s32[16,256]{1,0:T(8,128)} %add_add_fusion.tabr_ref, s32[256,6]{1,0:T(8,128)} %copy.23.tabc_ref), custom_call_target="tpu_custom_call" | custom-call | tf_op jit(solution)/shard_map/pallas_call | solution.py:536
  127.7 0.0 copy-start.1
  127.7 0.0 copy-start
  127.7 2.7 %copy.31 = f32[512,768]{1,0:T(8,128)} copy(f32[512,768]{1,0:T(8,128)} %get-tuple-element.16) | data formatting | bytes 3145728
  130.4 0.0 copy-done.1
  130.4 0.6 copy.32
  131.0 0.0 copy-done
  131.0 0.6 copy.33
  (3 shorter events, 0.0 us)
Async XLA Ops:
  127.7 2.7 %copy-start.1 = (f32[3,512]{1,0:T(4,128)S(1)}, f32[3,512]{1,0:T(4,128)}, u32[]{:S(2)}) copy-start(f32[3,512]{1,0:T(4,128)} %get-tuple-element.17) | copy-start | bytes 18436
  127.7 3.3 %copy-start = (f32[3,1024]{1,0:T(4,128)S(1)}, f32[3,1024]{1,0:T(4,128)}, u32[]{:S(2)}) copy-start(f32[3,1024]{1,0:T(4,128)} %get-tuple-element.18) | copy-start | bytes 36868

commit v2 on v1

v2 whole, which is shorter than its diff:
```python
import jax
import jax.numpy as jnp
from jax import lax
from jax.experimental import pallas as pl
from jax.experimental.pallas import tpu as pltpu
from jax.sharding import Mesh
from jax.sharding import PartitionSpec as P

F32 = jnp.float32
BF = jnp.bfloat16
I32 = jnp.int32
MESH = pl.DeviceIdType.MESH
HIGH = lax.Precision.HIGHEST

AXES = ("z", "y", "c", "x")
SIZE = {"z": 4, "y": 4, "c": 2, "x": 4}
ORDERS = (("x", "y", "z"), ("y", "z", "x"), ("z", "x", "y"))
PARTS = 3
ROWS = 1024
WIDTH = 768
SPLITS = 256
LEVELS = 3
FAR_FIRST = (2, 1, 3)
KIDS = 512
TILE = 128


def two(value):
    high = value.astype(BF)
    return high, (value - high.astype(F32)).astype(BF)


def dot(a, b):
    return jnp.dot(a, b, preferred_element_type=F32)


def aligned(value, step):
    return pl.multiple_of(value, step)


class Links:
    def __init__(self):
        self.me = {a: lax.axis_index(a) for a in AXES}
        self.started = []

    def at(self, axis, step):
        return lax.rem(self.me[axis] + step, SIZE[axis])

    def send(self, src, dst, send_sem, recv_sem, device):
        copy = pltpu.make_async_remote_copy(
            src_ref=src, dst_ref=dst, send_sem=send_sem, recv_sem=recv_sem, device_id=device, device_id_type=MESH
        )
        copy.start()
        self.started.append(copy)
        return copy

    def drain(self):
        for copy in self.started:
            copy.wait_send()
        self.started = []


def near_group(links):
    return [{"x": links.at("x", i), "c": links.at("c", j)} for i in range(4) for j in range(2) if i or j]


def far_group(links):
    return [{"z": links.at("z", i), "y": links.at("y", j)} for i in range(4) for j in range(4) if i or j]


class AllSum:
    def __init__(self, links, near, far, sems):
        self.links, self.near, self.far, self.sems = links, near, far, sems

    def start(self, rows):
        links = self.links
        slot = links.me["x"] * 2 + links.me["c"]
        for i, row in enumerate(rows):
            self.near[slot, i : i + 1, :] = row
        if len(rows) < 8:
            self.near[slot, len(rows) :, :] = jnp.zeros((8 - len(rows), SPLITS), F32)
        mine = self.near.at[slot]
        self.waits = [
            links.send(mine, mine, self.sems.at[0, k], self.sems.at[1, k], device)
            for k, device in enumerate(near_group(links))
        ]

    def middle(self):
        links = self.links
        for copy in self.waits:
            copy.wait_recv()
        total = self.near[0]
        for k in range(1, 8):
            total = total + self.near[k]
        slot = links.me["z"] * 4 + links.me["y"]
        self.far[slot] = total
        mine = self.far.at[slot]
        self.waits = [
            links.send(mine, mine, self.sems.at[0, 7 + k], self.sems.at[1, 7 + k], device)
            for k, device in enumerate(far_group(links))
        ]

    def finish(self):
        for copy in self.waits:
            copy.wait_recv()
        total = self.far[0]
        for k in range(1, 16):
            total = total + self.far[k]
        return total


def add_into(dst, first, rows, sources, step):
    @pl.loop(0, rows // step)
    def _(i):
        at = pl.ds(aligned(first + i * step, step), step)
        total = dst[at, :]
        for source in sources:
            total = total + source[pl.ds(aligned(i * step, step), step), :]
        dst[at, :] = total


class Scatter:
    def __init__(self, links, data, core, one, two_, three, sems):
        self.links, self.data, self.sems = links, data, sems
        self.core, self.one, self.two, self.three = core, one, two_, three
        self.waits = [[] for _ in range(PARTS)]

    def send(self, q, k, src, dst, device):
        self.waits[q].append(self.links.send(src, dst, self.sems.at[0, q, k], self.sems.at[1, q, k], device))

    def wait(self, q):
        for copy in self.waits[q]:
            copy.wait_recv()
        self.waits[q] = []

    def start_core(self, q):
        other = 1 - self.links.me["c"]
        src = self.data.at[pl.ds(aligned(256 * q + 128 * other, 128), 128), :]
        self.send(q, 0, src, self.core.at[q], {"c": other})

    def start_one(self):
        links = self.links
        for q in range(PARTS):
            self.wait(q)
            base = 256 * q + 128 * links.me["c"]
            add_into(self.data, base, 128, [self.core.at[q]], 16)
            axis = ORDERS[q][0]
            for k in FAR_FIRST:
                other = links.at(axis, k)
                src = self.data.at[pl.ds(aligned(base + 32 * other, 32), 32), :]
                self.send(q, k, src, self.one.at[q, k - 1], {axis: other})

    def start_two(self):
        links = self.links
        for q in range(PARTS):
            self.wait(q)
            base = 256 * q + 128 * links.me["c"] + 32 * links.me[ORDERS[q][0]]
            add_into(self.data, base, 32, [self.one.at[q, k] for k in range(3)], 8)
            axis = ORDERS[q][1]
            for k in FAR_FIRST:
                other = links.at(axis, k)
                src = self.data.at[pl.ds(aligned(base + 8 * other, 8), 8), :]
                self.send(q, 3 + k, src, self.two.at[q, k - 1], {axis: other})

    def start_three(self):
        links = self.links
        for q in range(PARTS):
            self.wait(q)
            base = own_row(links, q)
            axis = ORDERS[q][2]
            slot = links.me[axis]
            total = self.data[pl.ds(aligned(base, 8), 8), :]
            for k in range(3):
                total = total + self.two[q, k]
            self.three[q, slot] = total
            mine = self.three.at[q, slot]
            for k in FAR_FIRST:
                self.send(q, 6 + k, mine, mine, {axis: links.at(axis, k)})

    def finish(self, q):
        self.wait(q)
        return ((self.three[q, 0] + self.three[q, 1]) + self.three[q, 2]) + self.three[q, 3]

    def finish_all(self):
        return jnp.concatenate([self.finish(q) for q in range(PARTS)], axis=0)


def own_row(links, q):
    first, second, _ = ORDERS[q]
    return 256 * q + 128 * links.me["c"] + 32 * links.me[first] + 8 * links.me[second]


class Gather:
    def __init__(self, links, data, sems):
        self.links, self.data, self.sems = links, data, sems
        self.waits = [[] for _ in range(PARTS)]

    def push(self, q, k, base, rows, device):
        block = self.data.at[pl.ds(aligned(base, rows), rows), :]
        self.waits[q].append(self.links.send(block, block, self.sems.at[0, q, k], self.sems.at[1, q, k], device))

    def wait(self, q):
        for copy in self.waits[q]:
            copy.wait_recv()
        self.waits[q] = []

    def start_two(self, q, own):
        links = self.links
        base = own_row(links, q)
        self.data[pl.ds(aligned(base, 8), 8), :] = own
        axis = ORDERS[q][1]
        for k in FAR_FIRST:
            self.push(q, k, base, 8, {axis: links.at(axis, k)})

    def start_one(self):
        links = self.links
        for q in range(PARTS):
            self.wait(q)
            base = 256 * q + 128 * links.me["c"] + 32 * links.me[ORDERS[q][0]]
            axis = ORDERS[q][0]
            for k in FAR_FIRST:
                self.push(q, 3 + k, base, 32, {axis: links.at(axis, k)})

    def start_core(self):
        c = self.links.me["c"]
        for q in range(PARTS):
            self.wait(q)
            self.push(q, 0, 256 * q + 128 * c, 128, {"c": 1 - c})


def pick(index, columns):
    hit = lax.broadcasted_iota(I32, (SPLITS, SPLITS), 0) == index
    return [jnp.sum(jnp.where(hit, column, 0.0), axis=0, keepdims=True).astype(I32) for column in columns]


def kernel(e_hbm, root_hbm, mem_ref, split_ref, seed_ref, cent_hbm, spread_ref, cw_ref, *scratch):
    (
        e_ref, root_ref,
        eh, el, eth, etl, rh, rl, roott, oh, w_lo, dh, dl, proj, sq, memc, colt, cwbuf,
        xd, xu, x0, x1, x2, df, cf,
        core_d, core_u, core_0, core_1, core_2,
        one_d, one_u, one_0, one_1, one_2,
        two_d, two_u, two_0, two_1, two_2,
        three_d, three_u, three_0, three_1, three_2,
        near, far, woven, sem_rs, sem_ag, sem_ar, sem_in, sem_out,
    ) = scratch
    w_hi = oh
    links = Links()
    me = links.me
    barrier = pltpu.get_barrier_semaphore()
    peers = near_group(links) + far_group(links)
    for device in peers:
        pl.semaphore_signal(barrier, inc=1, device_id=device, device_id_type=MESH)

    tiles = ROWS // TILE

    def fetch(i):
        at = pl.ds(aligned(i * TILE, TILE), TILE)
        return pltpu.make_async_copy(e_hbm.at[at, :], e_ref.at[at, :], sem_in.at[i])

    root_copy = pltpu.make_async_copy(root_hbm, root_ref, sem_in.at[tiles])
    for i in range(tiles):
        fetch(i).start()
    root_copy.start()

    rs_d = Scatter(links, xd, core_d, one_d, two_d, three_d, sem_rs.at[0])
    rs_u = Scatter(links, xu, core_u, one_u, two_u, three_u, sem_rs.at[1])
    rs_0 = Scatter(links, x0, core_0, one_0, two_0, three_0, sem_rs.at[2])
    rs_1 = Scatter(links, x1, core_1, one_1, two_1, three_1, sem_rs.at[3])
    rs_2 = Scatter(links, x2, core_2, one_2, two_2, three_2, sem_rs.at[4])
    ag_d = Gather(links, df, sem_ag.at[0])
    ag_c = Gather(links, cf, sem_ag.at[1])
    sums = [AllSum(links, near.at[i], far.at[i], sem_ar.at[i]) for i in range(5)]

    first_row = (me["z"] * 32 + me["y"] * 8 + me["c"] * 4 + me["x"]) * ROWS
    splits = [split_ref[l : l + 1, :SPLITS] for l in range(LEVELS)]
    seed = [[seed_ref[l, j : j + 1, :] - first_row for j in range(2)] for l in range(LEVELS)]

    @pl.loop(0, tiles)
    def _(i):
        fetch(i).wait()
        at = pl.ds(aligned(i * TILE, TILE), TILE)
        rows = e_ref[at, :]
        high, low = two(rows)
        eh[at, :] = high
        el[at, :] = low
        sq[at, :] = jnp.sum(rows * rows, axis=1, keepdims=True)
        turned = jnp.transpose(rows)
        high, low = two(turned)
        eth[:, at] = high
        etl[:, at] = low

    def place(sign, with_norm):
        zero = jnp.zeros((1, SPLITS), F32)

        def body(i, carry):
            at = pl.ds(aligned(i * TILE, TILE), TILE)
            row = lax.broadcasted_iota(I32, (TILE, SPLITS), 0) + i * TILE
            out = []
            for l in range(LEVELS):
                value = jnp.where(row == seed[l][0], 1.0, 0.0) + jnp.where(row == seed[l][1], sign, 0.0)
                oh[at, l * SPLITS : (l + 1) * SPLITS] = value.astype(BF)
                if with_norm:
                    out.append(carry[l] + jnp.sum(value * sq[at, :], axis=0, keepdims=True))
            return tuple(out) if with_norm else carry

        return lax.fori_loop(0, tiles, body, (zero,) * LEVELS)

    def select_rows(dst, q):
        at = slice(256 * q, 256 * q + 256)
        dst[at, :] = dot(eth[at, :], oh[...]) + dot(etl[at, :], oh[...])

    norms = place(-1.0, True)
    select_rows(xd, 0)
    pl.semaphore_wait(barrier, len(peers))
    rs_d.start_core(0)
    sums[0].start(list(norms))
    for q in (1, 2):
        select_rows(xd, q)
        rs_d.start_core(q)

    lines = [splits[0], splits[1], seed_ref[0, 0:1, :], seed_ref[0, 1:2, :], seed_ref[1, 0:1, :], seed_ref[1, 1:2, :]]
    lines = [line.astype(F32) for line in lines] + [jnp.zeros((TILE - 6, SPLITS), F32)]
    colt[...] = jnp.transpose(jnp.concatenate(lines, axis=0))
    memc[...] = jnp.transpose(
        jnp.concatenate([mem_ref[...].astype(F32), jnp.zeros((TILE - LEVELS, ROWS), F32)], axis=0)
    )
    col = [colt[:, k : k + 1] for k in range(6)]
    kid1 = splits[1]
    a1, s10, s11 = pick(kid1 >> 1, [col[0], col[2], col[3]])
    odd1 = (kid1 & 1) == 1
    seed1 = jnp.where(odd1, s11, s10) - first_row
    kid2 = splits[2]
    mid2, s20, s21 = pick(kid2 >> 1, [col[1], col[4], col[5]])
    odd2 = (kid2 & 1) == 1
    seed2 = jnp.where(odd2, s21, s20) - first_row
    a2, t20, t21 = pick(mid2 >> 1, [col[0], col[2], col[3]])
    odd20 = (mid2 & 1) == 1
    seed20 = jnp.where(odd20, t21, t20) - first_row
    rs_d.start_one()

    root_copy.wait()

    @pl.loop(0, KIDS // TILE)
    def _(i):
        at = pl.ds(aligned(i * TILE, TILE), TILE)
        rows = root_ref[at, :]
        high, low = two(rows)
        rh[at, :] = high
        rl[at, :] = low
        roott[:, at] = jnp.transpose(rows)

    place(1.0, False)
    sums[0].middle()
    rs_d.start_two()
    select_rows(xu, 0)
    rs_d.start_three()
    select_rows(xu, 1)
    own_d = []
    for q in range(PARTS):
        own_d.append(rs_d.finish(q))
        ag_d.start_two(q, own_d[q])
    own_d = jnp.concatenate(own_d, axis=0)
    select_rows(xu, 2)
    ag_d.start_one()
    norm = sums[0].finish()
    ag_d.start_core()
    for q in range(PARTS):
        rs_u.start_core(q)

    for q in range(PARTS):
        ag_d.wait(q)
        for i in range(2):
            at = slice(256 * q + 128 * i, 256 * q + 128 * (i + 1))
            high, low = two(df[at, :])
            dh[at, :] = high
            dl[at, :] = low

    @pl.loop(0, ROWS // 256)
    def _(i):
        at = pl.ds(aligned(i * 256, 256), 256)
        proj[at, :] = dot(eh[at, :], dh[...]) + dot(eh[at, :], dl[...]) + dot(el[at, :], dh[...])

    rs_u.start_one()

    def root_body(i, carry):
        at = pl.ds(aligned(i * TILE, TILE), TILE)
        value = dot(rh[at, :], dh[...]) + dot(rh[at, :], dl[...]) + dot(rl[at, :], dh[...])
        row = lax.broadcasted_iota(I32, (TILE, SPLITS), 0) + i * TILE
        return tuple(
            carry[l] + jnp.sum(jnp.where(row == index, value[:, l * SPLITS : (l + 1) * SPLITS], 0.0), axis=0, keepdims=True)
            for l, index in enumerate((splits[0], a1, a2))
        )

    along = lax.fori_loop(0, KIDS // TILE, root_body, (jnp.zeros((1, SPLITS), F32),) * LEVELS)

    scale = 0.5 / float(WIDTH) ** 0.5

    def level(l, offset, chains):
        zero = jnp.zeros((1, SPLITS), F32)
        chains = [(cluster.astype(F32), odd, seed_row, ahead) for cluster, odd, seed_row, ahead in chains]
        own = splits[l].astype(F32)

        def body(i, carry):
            at = pl.ds(aligned(i * TILE, TILE), TILE)
            member = memc[at, l : l + 1]
            squares = sq[at, :]
            hit = member == own
            value = proj[at, l * SPLITS : (l + 1) * SPLITS] + offset
            gap = jnp.sum(jnp.where(hit, value, 0.0), axis=1, keepdims=True)
            inside = jnp.sum(jnp.where(hit, 1.0, 0.0), axis=1, keepdims=True)
            first = lax.logistic(gap * scale)
            second = 1.0 - first
            cwbuf[at, l : l + 1] = first * inside
            out = []
            for j, part in enumerate((first, second)):
                weight = jnp.where(hit, part, 0.0)
                high, low = two(weight)
                w_hi[at, j * SPLITS : (j + 1) * SPLITS] = high
                w_lo[at, j * SPLITS : (j + 1) * SPLITS] = low
                out.append(jnp.sum(weight, axis=0, keepdims=True))
                out.append(jnp.sum(weight * squares, axis=0, keepdims=True))
            row = lax.broadcasted_iota(I32, (TILE, SPLITS), 0) + i * TILE
            for cluster, odd, seed_row, ahead in chains:
                weight = jnp.where(member == cluster, jnp.where(odd, second, first), 0.0)
                both = weight + jnp.where(row == seed_row, 0.5, 0.0)
                out.append(jnp.sum(both * proj[at, ahead * SPLITS : (ahead + 1) * SPLITS], axis=0, keepdims=True))
                out.append(jnp.sum(weight, axis=0, keepdims=True))
            return tuple(a + b for a, b in zip(carry, out))

        return list(lax.fori_loop(0, tiles, body, (zero,) * (4 + 2 * len(chains))))

    def add_up(dst, q):
        at = slice(256 * q, 256 * q + 256)
        wide = w_hi[:, :KIDS]
        dst[at, :] = dot(eth[at, :], wide) + dot(etl[at, :], wide) + dot(eth[at, :], w_lo[...])

    offset = -0.5 * along[0] - 0.25 * norm[0:1, :]
    got0 = level(0, offset, [(a1, odd1, seed1, 1), (a2, odd20, seed20, 2)])
    sums[1].start(got0)
    add_up(x0, 0)
    add_up(x0, 1)
    sums[1].middle()
    rs_u.start_two()
    add_up(x0, 2)
    for q in range(PARTS):
        rs_0.start_core(q)
    got0 = sums[1].finish()

    rs_0.start_one()
    parent = (got0[4:5, :] + 0.5 * along[1]) / (got0[5:6, :] + 1.0)
    offset = -0.5 * parent - 0.25 * norm[1:2, :]
    got1 = level(1, offset, [(mid2, odd2, seed2, 2)])
    sums[2].start(got1)
    add_up(x1, 0)
    add_up(x1, 1)
    sums[2].middle()
    rs_u.start_three()
    rs_0.start_two()
    add_up(x1, 2)
    for q in range(PARTS):
        rs_1.start_core(q)
    got1 = sums[2].finish()

    rs_1.start_one()
    older = (got0[6:7, :] + 0.5 * along[2]) / (got0[7:8, :] + 1.0)
    parent = (got1[4:5, :] + 0.5 * older) / (got1[5:6, :] + 1.0)
    offset = -0.5 * parent - 0.25 * norm[2:3, :]
    got2 = level(2, offset, [])
    sums[3].start(got2)
    for q in range(PARTS):
        add_up(x2, q)
        rs_2.start_core(q)
    sums[3].middle()
    rs_2.start_one()
    rs_0.start_three()
    rs_1.start_two()
    cw_ref[...] = jnp.transpose(cwbuf[...])[0:LEVELS]
    own_u = rs_u.finish_all()
    rs_2.start_two()
    rs_1.start_three()

    def flat(kid):
        return (kid & 1) * SPLITS + (kid >> 1)

    def seeds_of(l, parent):
        up = own_u[:, l * SPLITS : (l + 1) * SPLITS]
        diff = own_d[:, l * SPLITS : (l + 1) * SPLITS]
        return 0.5 * jnp.concatenate([parent + 0.5 * (up + diff), parent + 0.5 * (up - diff)], axis=1)

    def parents(from_, kid):
        line = lax.broadcasted_iota(I32, (KIDS, SPLITS), 0)
        return jnp.dot(from_, jnp.where(line == kid, 1.0, 0.0).astype(F32), precision=HIGH, preferred_element_type=F32)

    def counts_of(got):
        return jnp.concatenate([got[0:1, :], got[2:3, :]], axis=1)

    def error_of(count, centre, mine):
        return 0.25 * jnp.sum(count * centre * centre - 2.0 * centre * mine, axis=0, keepdims=True)

    roots = jnp.concatenate([roott[pl.ds(aligned(own_row(links, q), 8), 8), :] for q in range(PARTS)], axis=0)
    n0, n1 = counts_of(got0), counts_of(got1)
    own_0 = rs_0.finish_all()
    c1 = (own_0 + seeds_of(0, parents(roots, splits[0]))) / (n0 + 1.0)
    err0 = error_of(n0, c1, own_0)
    got2 = sums[3].finish()
    n2 = counts_of(got2)
    rs_2.start_three()
    own_1 = rs_1.finish_all()
    c2 = (own_1 + seeds_of(1, parents(c1, flat(kid1)))) / (n1 + 1.0)
    err1 = error_of(n1, c2, own_1)
    seeds2 = seeds_of(2, parents(c2, flat(kid2)))
    part, err2 = [], 0.0
    for q in range(PARTS):
        mine = rs_2.finish(q)
        centre = (mine + seeds2[8 * q : 8 * q + 8]) / (n2 + 1.0)
        ag_c.start_two(q, centre)
        err2 = err2 + error_of(n2, centre, mine)
    sums[4].start([e[:, j * SPLITS : (j + 1) * SPLITS] for e in (err0, err1, err2) for j in range(2)])
    ag_c.start_one()
    sums[4].middle()
    ag_c.start_core()

    copies = []

    def weave(q, half):
        w = 2 * q + half
        rows = cf[pl.ds(aligned(TILE * w, TILE), TILE), :]
        for j in range(2):
            woven[w, pl.ds(j, SPLITS, stride=2), :] = jnp.transpose(rows[:, j * SPLITS : (j + 1) * SPLITS])
        copy = pltpu.make_async_copy(
            woven.at[w], cent_hbm.at[:, pl.ds(aligned(w * TILE, TILE), TILE)], sem_out.at[len(copies)]
        )
        copy.start()
        copies.append(copy)

    c = me["c"]
    for q in range(PARTS):
        weave(q, c)
    total = sums[4].finish()
    lines = []
    for l, (got, n) in enumerate(((got0, n0), (got1, n1), (got2, n2))):
        energy = jnp.concatenate([got[1:2, :], got[3:4, :]], axis=1)
        error = jnp.concatenate([total[2 * l : 2 * l + 1, :], total[2 * l + 1 : 2 * l + 2, :]], axis=1)
        lines.append((energy + error) / ((n + 1.0) * WIDTH))
    lines.append(jnp.zeros((8 - LEVELS, KIDS), F32))
    line = lax.broadcasted_iota(I32, (KIDS, KIDS), 0)
    kid = lax.broadcasted_iota(I32, (KIDS, KIDS), 1)
    order = jnp.where(line == flat(kid), 1.0, 0.0).astype(F32)
    spread_ref[...] = jnp.dot(
        jnp.concatenate(lines, axis=0), order, precision=HIGH, preferred_element_type=F32
    )[0:LEVELS]
    for q in range(PARTS):
        ag_c.wait(q)
        weave(q, 1 - c)
    for copy in copies:
        copy.wait()
    links.drain()


def scratch_shapes():
    vm = pltpu.VMEM
    widths = (WIDTH, WIDTH, KIDS, KIDS, KIDS)
    shapes = [
        vm((ROWS, WIDTH), F32), vm((KIDS, WIDTH), F32),
        vm((ROWS, WIDTH), BF), vm((ROWS, WIDTH), BF), vm((WIDTH, ROWS), BF), vm((WIDTH, ROWS), BF),
        vm((KIDS, WIDTH), BF), vm((KIDS, WIDTH), BF), vm((WIDTH, KIDS), F32),
        vm((ROWS, WIDTH), BF), vm((ROWS, KIDS), BF),
        vm((WIDTH, WIDTH), BF), vm((WIDTH, WIDTH), BF), vm((ROWS, WIDTH), F32),
        vm((ROWS, 1), F32), vm((ROWS, TILE), F32), vm((SPLITS, TILE), F32), vm((ROWS, TILE), F32),
    ]
    shapes += [vm((WIDTH, n), F32) for n in widths]
    shapes += [vm((WIDTH, WIDTH), F32), vm((WIDTH, KIDS), F32)]
    shapes += [vm((PARTS, 128, n), F32) for n in widths]
    shapes += [vm((PARTS, 3, 32, n), F32) for n in widths]
    shapes += [vm((PARTS, 3, 8, n), F32) for n in widths]
    shapes += [vm((PARTS, 4, 8, n), F32) for n in widths]
    dma = pltpu.SemaphoreType.DMA
    shapes += [vm((5, 8, 8, SPLITS), F32), vm((5, 16, 8, SPLITS), F32)]
    shapes += [vm((WIDTH // TILE, KIDS, TILE), F32)]
    shapes += [dma((5, 2, PARTS, 10)), dma((2, 2, PARTS, 7)), dma((5, 2, 22)), dma((ROWS // TILE + 1,)), dma((6,))]
    return shapes


def on_device(embeddings, root_centroids, member_ids, split_order, seed_rows):
    vmem = pl.BlockSpec(memory_space=pltpu.VMEM)
    hbm = pl.BlockSpec(memory_space=pl.ANY)
    return pl.pallas_call(
        kernel,
        out_shape=(
            jax.ShapeDtypeStruct((KIDS, WIDTH), F32),
            jax.ShapeDtypeStruct((LEVELS, KIDS), F32),
            jax.ShapeDtypeStruct((LEVELS, ROWS), F32),
        ),
        in_specs=[hbm, hbm, vmem, vmem, vmem],
        out_specs=(hbm, vmem, vmem),
        scratch_shapes=scratch_shapes(),
        compiler_params=pltpu.CompilerParams(
            collective_id=0, has_side_effects=True, vmem_limit_bytes=66_000_000
        ),
    )(embeddings, root_centroids, member_ids, split_order, seed_rows.transpose(0, 2, 1))


def solution(mesh):
    split = Mesh(mesh.devices.reshape(4, 4, 2, 4), AXES)
    everywhere = ("z", "y", "c", "x")
    in_specs = (P(everywhere, None), P(), P(None, everywhere), P(), P())
    out_specs = (P(), P(), P(None, everywhere))
    return jax.shard_map(on_device, mesh=split, in_specs=in_specs, out_specs=out_specs, check_vma=False)
```

time: 132 us -> 117 us (0.89)
  Pallas kernels: 121 us -> 112 us
  local copies, waits for them, and re-layouts: 9.51 us -> 3.87 us
    pallas_call x1, Pallas kernels: 121 us -> 112 us  [on_device(): pl.pallas_call(kernel, out_shape=(jax.ShapeDtypeStruct((KIDS, WIDTH), F32...]
    another operation x4 -> x0, local copies, waits for them, and re-layouts: 2.35 us -> none  [on_device(): jnp.stack([split_order[0, :SPLITS], split_order[1, :SPLITS], seed_rows[0,...]
    unnamed x8 -> x7, local copies, waits for them, and re-layouts: 5.61 us -> 3.87 us
    slice x2 -> x0, local copies, waits for them, and re-layouts: 1.46 us -> none  [the longest x1 0.77 us: on_device(): seed_rows[:, :, 0]]
where the time goes in v2:
time: 117 us
  Pallas kernels  112 us (96%)
  local copies, waits for them, and re-layouts  3.87 us (3%)
    pallas_call x1, Pallas kernels, on_device(): pl.pallas_call(kernel, out_shape=(jax.ShapeDtypeStruct((KIDS, WIDTH), F32...  112 us
    unnamed x7, local copies, waits for them, and re-layouts  3.87 us

profile of v2, /device:TPU:1, one launch (start us, length us, event | category | flops | bytes accessed | tf_op | source)
XLA Modules:
  0.0 116.8 jit_solution(93660252222735447)
XLA Ops:
  0.6 112.2 %shard_map.76 = (f32[512,768]{1,0:T(8,128)}, f32[3,512]{1,0:T(4,128)}, f32[3,1024]{1,0:T(4,128)}) custom-call(f32[1024,768]{1,0:T(8,128)} %e_hbm.1, f32[512,768]{1,0:T(8,128)} %root_hbm.1, s32[3,1024]{1,0:T(4,128)} %mem_ref.1, s32[3,512]{1,0:T(4,128)} %split_ref.1, s32[3,2,256]{2,1,0:T(2,128)} %bitcast.1), custom_call_target="tpu_custom_call" | custom-call | tf_op jit(solution)/shard_map/pallas_call | solution.py:588
  112.9 0.0 copy-start.1
  112.9 0.0 copy-start
  112.9 2.7 %copy.11 = f32[512,768]{1,0:T(8,128)} copy(f32[512,768]{1,0:T(8,128)} %get-tuple-element.6) | data formatting | bytes 3145728
  115.6 0.0 copy-done.1
  115.6 0.6 copy.12
  116.2 0.0 copy-done
  116.2 0.6 copy.13
Async XLA Ops:
  112.9 2.7 %copy-start.1 = (f32[3,512]{1,0:T(4,128)S(1)}, f32[3,512]{1,0:T(4,128)}, u32[]{:S(2)}) copy-start(f32[3,512]{1,0:T(4,128)} %get-tuple-element.7) | copy-start | bytes 18436
  112.9 3.3 %copy-start = (f32[3,1024]{1,0:T(4,128)S(1)}, f32[3,1024]{1,0:T(4,128)}, u32[]{:S(2)}) copy-start(f32[3,1024]{1,0:T(4,128)} %get-tuple-element.8) | copy-start | bytes 36868

commit v3 on v2

--- a/solution.py
+++ b/solution.py
@@ -138,44 +138,45 @@
         src = self.data.at[pl.ds(aligned(256 * q + 128 * other, 128), 128), :]
         self.send(q, 0, src, self.core.at[q], {"c": other})
 
-    def start_one(self):
+    def start_one(self, q):
         links = self.links
+        self.wait(q)
+        base = 256 * q + 128 * links.me["c"]
+        add_into(self.data, base, 128, [self.core.at[q]], 16)
+        axis = ORDERS[q][0]
+        for k in FAR_FIRST:
+            other = links.at(axis, k)
+            src = self.data.at[pl.ds(aligned(base + 32 * other, 32), 32), :]
+            self.send(q, k, src, self.one.at[q, k - 1], {axis: other})
+
+    def start_two(self, q):
+        links = self.links
+        self.wait(q)
+        base = 256 * q + 128 * links.me["c"] + 32 * links.me[ORDERS[q][0]]
+        add_into(self.data, base, 32, [self.one.at[q, k] for k in range(3)], 8)
+        axis = ORDERS[q][1]
+        for k in FAR_FIRST:
+            other = links.at(axis, k)
+            src = self.data.at[pl.ds(aligned(base + 8 * other, 8), 8), :]
+            self.send(q, 3 + k, src, self.two.at[q, k - 1], {axis: other})
+
+    def start_three(self, q):
+        links = self.links
+        self.wait(q)
+        base = own_row(links, q)
+        axis = ORDERS[q][2]
+        slot = links.me[axis]
+        total = self.data[pl.ds(aligned(base, 8), 8), :]
+        for k in range(3):
+            total = total + self.two[q, k]
+        self.three[q, slot] = total
+        mine = self.three.at[q, slot]
+        for k in FAR_FIRST:
+            self.send(q, 6 + k, mine, mine, {axis: links.at(axis, k)})
+
+    def every(self, step):
         for q in range(PARTS):
-            self.wait(q)
-            base = 256 * q + 128 * links.me["c"]
-            add_into(self.data, base, 128, [self.core.at[q]], 16)
-            axis = ORDERS[q][0]
-            for k in FAR_FIRST:
-                other = links.at(axis, k)
-                src = self.data.at[pl.ds(aligned(base + 32 * other, 32), 32), :]
-                self.send(q, k, src, self.one.at[q, k - 1], {axis: other})
-
-    def start_two(self):
-        links = self.links
-        for q in range(PARTS):
-            self.wait(q)
-            base = 256 * q + 128 * links.me["c"] + 32 * links.me[ORDERS[q][0]]
-            add_into(self.data, base, 32, [self.one.at[q, k] for k in range(3)], 8)
-            axis = ORDERS[q][1]
-            for k in FAR_FIRST:
-                other = links.at(axis, k)
-                src = self.data.at[pl.ds(aligned(base + 8 * other, 8), 8), :]
-                self.send(q, 3 + k, src, self.two.at[q, k - 1], {axis: other})
-
-    def start_three(self):
-        links = self.links
-        for q in range(PARTS):
-            self.wait(q)
-            base = own_row(links, q)
-            axis = ORDERS[q][2]
-            slot = links.me[axis]
-            total = self.data[pl.ds(aligned(base, 8), 8), :]
-            for k in range(3):
-                total = total + self.two[q, k]
-            self.three[q, slot] = total
-            mine = self.three.at[q, slot]
-            for k in FAR_FIRST:
-                self.send(q, 6 + k, mine, mine, {axis: links.at(axis, k)})
+            step(q)
 
     def finish(self, q):
         self.wait(q)
@@ -236,7 +237,7 @@
 def kernel(e_hbm, root_hbm, mem_ref, split_ref, seed_ref, cent_hbm, spread_ref, cw_ref, *scratch):
     (
         e_ref, root_ref,
-        eh, el, eth, etl, rh, rl, roott, oh, w_lo, dh, dl, proj, sq, memc, colt, cwbuf,
+        eh, el, eth, etl, rh, rl, roott, oh, w_lo, dh, dl, proj, sq, memc, colt, cwbuf, firsts,
         xd, xu, x0, x1, x2, df, cf,
         core_d, core_u, core_0, core_1, core_2,
         one_d, one_u, one_0, one_1, one_2,
@@ -276,48 +277,50 @@
     splits = [split_ref[l : l + 1, :SPLITS] for l in range(LEVELS)]
     seed = [[seed_ref[l, j : j + 1, :] - first_row for j in range(2)] for l in range(LEVELS)]
 
+    def place(sign):
+        @pl.loop(0, tiles)
+        def _(i):
+            at = pl.ds(aligned(i * TILE, TILE), TILE)
+            row = lax.broadcasted_iota(I32, (TILE, SPLITS), 0) + i * TILE
+            for l in range(LEVELS):
+                value = jnp.where(row == seed[l][0], 1.0, 0.0) + jnp.where(row == seed[l][1], sign, 0.0)
+                oh[at, l * SPLITS : (l + 1) * SPLITS] = value.astype(BF)
+
+    place(-1.0)
+
     @pl.loop(0, tiles)
     def _(i):
         fetch(i).wait()
+        at = pl.ds(aligned(i * TILE, TILE), TILE)
+        high, low = two(jnp.transpose(e_ref[at, :]))
+        eth[:, at] = high
+        etl[:, at] = low
+
+    def as_they_lie(i, carry):
         at = pl.ds(aligned(i * TILE, TILE), TILE)
         rows = e_ref[at, :]
         high, low = two(rows)
         eh[at, :] = high
         el[at, :] = low
-        sq[at, :] = jnp.sum(rows * rows, axis=1, keepdims=True)
-        turned = jnp.transpose(rows)
-        high, low = two(turned)
-        eth[:, at] = high
-        etl[:, at] = low
-
-    def place(sign, with_norm):
-        zero = jnp.zeros((1, SPLITS), F32)
-
-        def body(i, carry):
-            at = pl.ds(aligned(i * TILE, TILE), TILE)
-            row = lax.broadcasted_iota(I32, (TILE, SPLITS), 0) + i * TILE
-            out = []
-            for l in range(LEVELS):
-                value = jnp.where(row == seed[l][0], 1.0, 0.0) + jnp.where(row == seed[l][1], sign, 0.0)
-                oh[at, l * SPLITS : (l + 1) * SPLITS] = value.astype(BF)
-                if with_norm:
-                    out.append(carry[l] + jnp.sum(value * sq[at, :], axis=0, keepdims=True))
-            return tuple(out) if with_norm else carry
-
-        return lax.fori_loop(0, tiles, body, (zero,) * LEVELS)
+        squares = jnp.sum(rows * rows, axis=1, keepdims=True)
+        sq[at, :] = squares
+        return tuple(
+            carry[l] + jnp.sum(oh[at, l * SPLITS : (l + 1) * SPLITS].astype(F32) * squares, axis=0, keepdims=True)
+            for l in range(LEVELS)
+        )
 
     def select_rows(dst, q):
         at = slice(256 * q, 256 * q + 256)
         dst[at, :] = dot(eth[at, :], oh[...]) + dot(etl[at, :], oh[...])
 
-    norms = place(-1.0, True)
     select_rows(xd, 0)
     pl.semaphore_wait(barrier, len(peers))
     rs_d.start_core(0)
-    sums[0].start(list(norms))
-    for q in (1, 2):
-        select_rows(xd, q)
-        rs_d.start_core(q)
+    select_rows(xd, 1)
+    rs_d.start_core(1)
+    select_rows(xd, 2)
+    rs_d.start_core(2)
+    rs_d.start_one(0)
 
     lines = [splits[0], splits[1], seed_ref[0, 0:1, :], seed_ref[0, 1:2, :], seed_ref[1, 0:1, :], seed_ref[1, 1:2, :]]
     lines = [line.astype(F32) for line in lines] + [jnp.zeros((TILE - 6, SPLITS), F32)]
@@ -337,7 +340,10 @@
     a2, t20, t21 = pick(mid2 >> 1, [col[0], col[2], col[3]])
     odd20 = (mid2 & 1) == 1
     seed20 = jnp.where(odd20, t21, t20) - first_row
-    rs_d.start_one()
+    rs_d.start_one(1)
+    rs_d.start_one(2)
+    norms = lax.fori_loop(0, tiles, as_they_lie, (jnp.zeros((1, SPLITS), F32),) * LEVELS)
+    sums[0].start(list(norms))
 
     root_copy.wait()
 
@@ -350,11 +356,11 @@
         rl[at, :] = low
         roott[:, at] = jnp.transpose(rows)
 
-    place(1.0, False)
+    place(1.0)
     sums[0].middle()
-    rs_d.start_two()
+    rs_d.every(rs_d.start_two)
     select_rows(xu, 0)
-    rs_d.start_three()
+    rs_d.every(rs_d.start_three)
     select_rows(xu, 1)
     own_d = []
     for q in range(PARTS):
@@ -376,23 +382,31 @@
             dh[at, :] = high
             dl[at, :] = low
 
-    @pl.loop(0, ROWS // 256)
-    def _(i):
-        at = pl.ds(aligned(i * 256, 256), 256)
-        proj[at, :] = dot(eh[at, :], dh[...]) + dot(eh[at, :], dl[...]) + dot(el[at, :], dh[...])
-
-    rs_u.start_one()
-
-    def root_body(i, carry):
-        at = pl.ds(aligned(i * TILE, TILE), TILE)
-        value = dot(rh[at, :], dh[...]) + dot(rh[at, :], dl[...]) + dot(rl[at, :], dh[...])
-        row = lax.broadcasted_iota(I32, (TILE, SPLITS), 0) + i * TILE
-        return tuple(
-            carry[l] + jnp.sum(jnp.where(row == index, value[:, l * SPLITS : (l + 1) * SPLITS], 0.0), axis=0, keepdims=True)
-            for l, index in enumerate((splits[0], a1, a2))
-        )
-
-    along = lax.fori_loop(0, KIDS // TILE, root_body, (jnp.zeros((1, SPLITS), F32),) * LEVELS)
+    def products(first):
+        @pl.loop(first, first + 2)
+        def _(i):
+            at = pl.ds(aligned(i * 256, 256), 256)
+            proj[at, :] = dot(eh[at, :], dh[...]) + dot(eh[at, :], dl[...]) + dot(el[at, :], dh[...])
+
+    products(0)
+    rs_u.every(rs_u.start_one)
+    products(2)
+
+    def root_products(levels, indices):
+        cols = slice(levels[0] * SPLITS, (levels[-1] + 1) * SPLITS)
+
+        def body(i, carry):
+            at = pl.ds(aligned(i * TILE, TILE), TILE)
+            value = dot(rh[at, :], dh[:, cols]) + dot(rh[at, :], dl[:, cols]) + dot(rl[at, :], dh[:, cols])
+            row = lax.broadcasted_iota(I32, (TILE, SPLITS), 0) + i * TILE
+            return tuple(
+                carry[k] + jnp.sum(jnp.where(row == index, value[:, k * SPLITS : (k + 1) * SPLITS], 0.0), axis=0, keepdims=True)
+                for k, index in enumerate(indices)
+            )
+
+        return lax.fori_loop(0, KIDS // TILE, body, (jnp.zeros((1, SPLITS), F32),) * len(levels))
+
+    along0 = root_products([0], [splits[0]])[0]
 
     scale = 0.5 / float(WIDTH) ** 0.5
 
@@ -404,22 +418,12 @@
         def body(i, carry):
             at = pl.ds(aligned(i * TILE, TILE), TILE)
             member = memc[at, l : l + 1]
-            squares = sq[at, :]
-            hit = member == own
             value = proj[at, l * SPLITS : (l + 1) * SPLITS] + offset
-            gap = jnp.sum(jnp.where(hit, value, 0.0), axis=1, keepdims=True)
-            inside = jnp.sum(jnp.where(hit, 1.0, 0.0), axis=1, keepdims=True)
+            gap = jnp.sum(jnp.where(member == own, value, 0.0), axis=1, keepdims=True)
             first = lax.logistic(gap * scale)
             second = 1.0 - first
-            cwbuf[at, l : l + 1] = first * inside
+            firsts[at, :] = first
             out = []
-            for j, part in enumerate((first, second)):
-                weight = jnp.where(hit, part, 0.0)
-                high, low = two(weight)
-                w_hi[at, j * SPLITS : (j + 1) * SPLITS] = high
-                w_lo[at, j * SPLITS : (j + 1) * SPLITS] = low
-                out.append(jnp.sum(weight, axis=0, keepdims=True))
-                out.append(jnp.sum(weight * squares, axis=0, keepdims=True))
             row = lax.broadcasted_iota(I32, (TILE, SPLITS), 0) + i * TILE
             for cluster, odd, seed_row, ahead in chains:
                 weight = jnp.where(member == cluster, jnp.where(odd, second, first), 0.0)
@@ -428,57 +432,93 @@
                 out.append(jnp.sum(weight, axis=0, keepdims=True))
             return tuple(a + b for a, b in zip(carry, out))
 
-        return list(lax.fori_loop(0, tiles, body, (zero,) * (4 + 2 * len(chains))))
-
-    def add_up(dst, q):
-        at = slice(256 * q, 256 * q + 256)
-        wide = w_hi[:, :KIDS]
-        dst[at, :] = dot(eth[at, :], wide) + dot(etl[at, :], wide) + dot(eth[at, :], w_lo[...])
-
-    offset = -0.5 * along[0] - 0.25 * norm[0:1, :]
+        return list(lax.fori_loop(0, tiles, body, (zero,) * (2 * len(chains))))
+
+    def weigh(l):
+        zero = jnp.zeros((1, SPLITS), F32)
+        own = splits[l].astype(F32)
+
+        def body(i, carry):
+            at = pl.ds(aligned(i * TILE, TILE), TILE)
+            hit = memc[at, l : l + 1] == own
+            first = firsts[at, :]
+            squares = sq[at, :]
+            inside = jnp.sum(jnp.where(hit, 1.0, 0.0), axis=1, keepdims=True)
+            cwbuf[at, l : l + 1] = first * inside
+            out = []
+            for j, part in enumerate((first, 1.0 - first)):
+                weight = jnp.where(hit, part, 0.0)
+                high, low = two(weight)
+                w_hi[at, j * SPLITS : (j + 1) * SPLITS] = high
+                w_lo[at, j * SPLITS : (j + 1) * SPLITS] = low
+                out.append(jnp.sum(weight, axis=0, keepdims=True))
+                out.append(jnp.sum(weight * squares, axis=0, keepdims=True))
+            return tuple(a + b for a, b in zip(carry, out))
+
+        return list(lax.fori_loop(0, tiles, body, (zero,) * 4))
+
+    def add_up(dst, q, j):
+        at, cols = slice(256 * q, 256 * q + 256), slice(SPLITS * j, SPLITS * j + SPLITS)
+        high = w_hi[:, cols]
+        dst[at, cols] = dot(eth[at, :], high) + dot(etl[at, :], high) + dot(eth[at, :], w_lo[:, cols])
+
+    offset = -0.5 * along0 - 0.25 * norm[0:1, :]
     got0 = level(0, offset, [(a1, odd1, seed1, 1), (a2, odd20, seed20, 2)])
     sums[1].start(got0)
-    add_up(x0, 0)
-    add_up(x0, 1)
+    tally0 = weigh(0)
+    add_up(x0, 0, 0)
     sums[1].middle()
-    rs_u.start_two()
-    add_up(x0, 2)
-    for q in range(PARTS):
+    along1, along2 = root_products([1, 2], [a1, a2])
+    add_up(x0, 0, 1)
+    rs_0.start_core(0)
+    for q in (1, 2):
+        for j in (0, 1):
+            add_up(x0, q, j)
         rs_0.start_core(q)
     got0 = sums[1].finish()
 
-    rs_0.start_one()
-    parent = (got0[4:5, :] + 0.5 * along[1]) / (got0[5:6, :] + 1.0)
+    parent = (got0[0:1, :] + 0.5 * along1) / (got0[1:2, :] + 1.0)
     offset = -0.5 * parent - 0.25 * norm[1:2, :]
     got1 = level(1, offset, [(mid2, odd2, seed2, 2)])
-    sums[2].start(got1)
-    add_up(x1, 0)
-    add_up(x1, 1)
+    sums[2].start(got1 + tally0)
+    tally1 = weigh(1)
+    rs_u.every(rs_u.start_two)
+    add_up(x1, 0, 0)
     sums[2].middle()
-    rs_u.start_three()
-    rs_0.start_two()
-    add_up(x1, 2)
+    add_up(x1, 0, 1)
+    rs_1.start_core(0)
+    add_up(x1, 1, 0)
+    rs_0.every(rs_0.start_one)
+    add_up(x1, 1, 1)
+    rs_1.start_core(1)
+    add_up(x1, 2, 0)
+    add_up(x1, 2, 1)
+    rs_1.start_core(2)
+    got1 = sums[2].finish()
+
+    rs_1.every(rs_1.start_one)
+    older = (got0[2:3, :] + 0.5 * along2) / (got0[3:4, :] + 1.0)
+    parent = (got1[0:1, :] + 0.5 * older) / (got1[1:2, :] + 1.0)
+    offset = -0.5 * parent - 0.25 * norm[2:3, :]
+    level(2, offset, [])
+    tally2 = weigh(2)
+    sums[3].start(tally1 + tally2)
     for q in range(PARTS):
-        rs_1.start_core(q)
-    got1 = sums[2].finish()
-
-    rs_1.start_one()
-    older = (got0[6:7, :] + 0.5 * along[2]) / (got0[7:8, :] + 1.0)
-    parent = (got1[4:5, :] + 0.5 * older) / (got1[5:6, :] + 1.0)
-    offset = -0.5 * parent - 0.25 * norm[2:3, :]
-    got2 = level(2, offset, [])
-    sums[3].start(got2)
-    for q in range(PARTS):
-        add_up(x2, q)
+        for j in (0, 1):
+            add_up(x2, q, j)
         rs_2.start_core(q)
+        if q:
+            rs_2.start_one(q - 1)
+    rs_2.start_one(2)
     sums[3].middle()
-    rs_2.start_one()
-    rs_0.start_three()
-    rs_1.start_two()
+    rs_u.every(rs_u.start_three)
+    rs_0.every(rs_0.start_two)
+    rs_1.every(rs_1.start_two)
     cw_ref[...] = jnp.transpose(cwbuf[...])[0:LEVELS]
     own_u = rs_u.finish_all()
-    rs_2.start_two()
-    rs_1.start_three()
+    rs_2.every(rs_2.start_two)
+    rs_0.every(rs_0.start_three)
+    rs_1.every(rs_1.start_three)
 
     def flat(kid):
         return (kid & 1) * SPLITS + (kid >> 1)
@@ -499,13 +539,15 @@
         return 0.25 * jnp.sum(count * centre * centre - 2.0 * centre * mine, axis=0, keepdims=True)
 
     roots = jnp.concatenate([roott[pl.ds(aligned(own_row(links, q), 8), 8), :] for q in range(PARTS)], axis=0)
-    n0, n1 = counts_of(got0), counts_of(got1)
+    got0 = got1[2:6, :]
+    n0 = counts_of(got0)
     own_0 = rs_0.finish_all()
     c1 = (own_0 + seeds_of(0, parents(roots, splits[0]))) / (n0 + 1.0)
     err0 = error_of(n0, c1, own_0)
     got2 = sums[3].finish()
-    n2 = counts_of(got2)
-    rs_2.start_three()
+    got1, got2 = got2[0:4, :], got2[4:8, :]
+    n1, n2 = counts_of(got1), counts_of(got2)
+    rs_2.every(rs_2.start_three)
     own_1 = rs_1.finish_all()
     c2 = (own_1 + seeds_of(1, parents(c1, flat(kid1)))) / (n1 + 1.0)
     err1 = error_of(n1, c2, own_1)
@@ -567,7 +609,7 @@
         vm((KIDS, WIDTH), BF), vm((KIDS, WIDTH), BF), vm((WIDTH, KIDS), F32),
         vm((ROWS, WIDTH), BF), vm((ROWS, KIDS), BF),
         vm((WIDTH, WIDTH), BF), vm((WIDTH, WIDTH), BF), vm((ROWS, WIDTH), F32),
-        vm((ROWS, 1), F32), vm((ROWS, TILE), F32), vm((SPLITS, TILE), F32), vm((ROWS, TILE), F32),
+        vm((ROWS, 1), F32), vm((ROWS, TILE), F32), vm((SPLITS, TILE), F32), vm((ROWS, TILE), F32), vm((ROWS, 1), F32),
     ]
     shapes += [vm((WIDTH, n), F32) for n in widths]
     shapes += [vm((WIDTH, WIDTH), F32), vm((WIDTH, KIDS), F32)]

time: 117 us -> 115 us (0.983)
    pallas_call x1, Pallas kernels: 112 us -> 111 us  [on_device(): pl.pallas_call(kernel, out_shape=(jax.ShapeDtypeStruct((KIDS, WIDTH), F32...]
where the time goes in v3:
time: 115 us
  Pallas kernels  111 us (97%)
  local copies, waits for them, and re-layouts  3.87 us (3%)
    pallas_call x1, Pallas kernels, on_device(): pl.pallas_call(kernel, out_shape=(jax.ShapeDtypeStruct((KIDS, WIDTH), F32...  111 us
    unnamed x7, local copies, waits for them, and re-layouts  3.87 us

profile of v3, /device:TPU:1, one launch (start us, length us, event | category | flops | bytes accessed | tf_op | source)
XLA Modules:
  0.0 115.1 jit_solution(1226209357356741168)
XLA Ops:
  0.6 110.6 %shard_map.76 = (f32[512,768]{1,0:T(8,128)}, f32[3,512]{1,0:T(4,128)}, f32[3,1024]{1,0:T(4,128)}) custom-call(f32[1024,768]{1,0:T(8,128)} %e_hbm.1, f32[512,768]{1,0:T(8,128)} %root_hbm.1, s32[3,1024]{1,0:T(4,128)} %mem_ref.1, s32[3,512]{1,0:T(4,128)} %split_ref.1, s32[3,2,256]{2,1,0:T(2,128)} %bitcast.1), custom_call_target="tpu_custom_call" | custom-call | tf_op jit(solution)/shard_map/pallas_call | solution.py:630
  111.2 0.0 copy-start.1
  111.2 0.0 copy-start
  111.2 2.7 %copy.11 = f32[512,768]{1,0:T(8,128)} copy(f32[512,768]{1,0:T(8,128)} %get-tuple-element.6) | data formatting | bytes 3145728
  113.9 0.0 copy-done.1
  113.9 0.6 copy.12
  114.5 0.0 copy-done
  114.5 0.6 copy.13
Async XLA Ops:
  111.2 2.7 %copy-start.1 = (f32[3,512]{1,0:T(4,128)S(1)}, f32[3,512]{1,0:T(4,128)}, u32[]{:S(2)}) copy-start(f32[3,512]{1,0:T(4,128)} %get-tuple-element.7) | copy-start | bytes 18436
  111.2 3.3 %copy-start = (f32[3,1024]{1,0:T(4,128)S(1)}, f32[3,1024]{1,0:T(4,128)}, u32[]{:S(2)}) copy-start(f32[3,1024]{1,0:T(4,128)} %get-tuple-element.8) | copy-start | bytes 36868

commit v4 on v3

--- a/solution.py
+++ b/solution.py
@@ -624,10 +624,36 @@
     return shapes
 
 
+def hand_on_kernel(cent_ref, spread_ref, cw_ref, cent_out, spread_out, cw_out):
+    cent_out[...] = cent_ref[...]
+
+    @pl.when(pl.program_id(0) == 0)
+    def _():
+        spread_out[...] = spread_ref[...]
+        cw_out[...] = cw_ref[...]
+
+
+def hand_on(*results):
+    steps = 2
+    specs = [
+        pl.BlockSpec((KIDS // steps, WIDTH), lambda i: (i, 0)),
+        pl.BlockSpec((LEVELS, KIDS), lambda i: (0, 0)),
+        pl.BlockSpec((LEVELS, ROWS), lambda i: (0, 0)),
+    ]
+    return pl.pallas_call(
+        hand_on_kernel,
+        grid=(steps,),
+        out_shape=tuple(jax.ShapeDtypeStruct(r.shape, r.dtype) for r in results),
+        in_specs=specs,
+        out_specs=tuple(specs),
+        compiler_params=pltpu.CompilerParams(vmem_limit_bytes=66_000_000),
+    )(*results)
+
+
 def on_device(embeddings, root_centroids, member_ids, split_order, seed_rows):
     vmem = pl.BlockSpec(memory_space=pltpu.VMEM)
     hbm = pl.BlockSpec(memory_space=pl.ANY)
-    return pl.pallas_call(
+    results = pl.pallas_call(
         kernel,
         out_shape=(
             jax.ShapeDtypeStruct((KIDS, WIDTH), F32),
@@ -641,6 +667,7 @@
             collective_id=0, has_side_effects=True, vmem_limit_bytes=66_000_000
         ),
     )(embeddings, root_centroids, member_ids, split_order, seed_rows.transpose(0, 2, 1))
+    return hand_on(*results)
 
 
 def solution(mesh):

time: 115 us -> 114 us (level)
  local copies, waits for them, and re-layouts: 3.87 us -> 0 us
  Pallas kernels: 111 us -> 113 us
    unnamed x7 -> x0, local copies, waits for them, and re-layouts: 3.87 us -> none
    pallas_call x0 -> x1, Pallas kernels: none -> 2.36 us  [hand_on(): pl.pallas_call(hand_on_kernel, grid=(steps,), out_shape=tuple((jax.ShapeD...]
where the time goes in v4:
time: 114 us
  Pallas kernels  113 us (99%)
    pallas_call x1, Pallas kernels, on_device(): pl.pallas_call(kernel, out_shape=(jax.ShapeDtypeStruct((KIDS, WIDTH), F32...  111 us
    pallas_call x1, Pallas kernels, hand_on(): pl.pallas_call(hand_on_kernel, grid=(steps,), out_shape=tuple((jax.ShapeD...  2.36 us

profile of v4, /device:TPU:1, one launch (start us, length us, event | category | flops | bytes accessed | tf_op | source)
XLA Modules:
  0.0 113.6 jit_solution(9512389012496754000)
XLA Ops:
  0.6 110.6 %shard_map.76 = (f32[512,768]{1,0:T(8,128)}, f32[3,512]{1,0:T(4,128)}, f32[3,1024]{1,0:T(4,128)}) custom-call(f32[1024,768]{1,0:T(8,128)} %e_hbm.1, f32[512,768]{1,0:T(8,128)} %root_hbm.1, s32[3,1024]{1,0:T(4,128)} %mem_ref.1, s32[3,512]{1,0:T(4,128)} %split_ref.1, s32[3,2,256]{2,1,0:T(2,128)} %bitcast.1), custom_call_target="tpu_custom_call" | custom-call | tf_op jit(solution)/shard_map/pallas_call | solution.py:656
  111.2 2.4 %shard_map.77 = (f32[512,768]{1,0:T(8,128)}, f32[3,512]{1,0:T(4,128)}, f32[3,1024]{1,0:T(4,128)}) custom-call(f32[512,768]{1,0:T(8,128)} %get-tuple-element.6.cent_ref, f32[3,512]{1,0:T(4,128)} %get-tuple-element.7.spread_ref, f32[3,1024]{1,0:T(4,128)} %get-tuple-element.8.cw_ref), custom_call_target="tpu_custom_call" | custom-call | tf_op jit(solution)/shard_map/pallas_call | solution.py:643
